TPU v7x, 32 devices: a whole 2x2x4 slice. The times are simulated.
32 devices in a mesh: grp: 2 (over y), ep: 4 (over z), hd: 2 (over x), sub: 2 (over core).
Axes of the slice: x: 2, y: 2, z: 4, core: 2. Of those that a mesh axis runs over, the one named last changes fastest.
Arguments:
- queries: bfloat16 [2048, 4096], P(('grp', 'ep'), 'hd'), parts along dimension 0, may hold values from -1024 to 1024
- cache_keys: bfloat16 [2048, 512], P(('grp', 'ep', 'sub')), parts along dimension 0, may hold values from -4 to 4
- cache_values: bfloat16 [2048, 512], P(('grp', 'ep', 'sub')), parts along dimension 0, may hold values from -12 to 12
- page_len: int32 [16], P(('grp', 'ep', 'sub')), parts along dimension 0, may hold values from 1 to 128, 512 in all
- new_keys: bfloat16 [2048, 512], P(('grp', 'ep', 'sub')), parts along dimension 0, may hold values from -6 to 6
- new_values: bfloat16 [2048, 512], P(('grp', 'ep', 'sub')), parts along dimension 0, may hold values from -6 to 6
- out_proj: bfloat16 [4096, 2048], P('hd', 'sub'), may hold values from -0.09375 to 0.09375
- residual: bfloat16 [2048, 2048], P(('grp', 'ep', 'hd'), 'sub'), parts along dimension 0, may hold values from -6 to 6
- norm_gain: bfloat16 [2048], replicated, may hold values from 0.099609375 to 1.8984375
- gate_up: bfloat16 [8, 2, 384, 2048], P(('ep', 'hd'), None, 'sub'), may hold values from -0.125 to 0.125
- w_down: bfloat16 [8, 384, 2048], P(('ep', 'hd'), 'sub'), may hold values from -0.3125 to 0.3125
- expert_ids: int32 [2048, 8], P(('grp', 'ep', 'hd')), parts along dimension 0, may hold values from 0 to 7, as said below
- gates: bfloat16 [2048, 8], P(('grp', 'ep', 'hd')), parts along dimension 0, may hold values from 0.049804688 to 0.5
Outputs:
- layer_out: bfloat16 [2048, 2048], P(('grp', 'ep', 'hd'), 'sub'), parts along dimension 0
There are 2 independent parts, one for each index of `grp`. A program takes and returns all parts, laid end to end along the dimension named above; an argument that names none is the same for every part. Nothing has to cross between parts.
Inputs may be any that keep to these rules, and one draw needn't show every extreme that they name: `expert_ids`: expert x belongs to group x // 2. Each row names 8 different experts, exactly two in each of 4 different groups. Among the rows of one block b (rows b * 128 to (b + 1) * 128 - 1), each group is named by at most 128 rows and each expert by at most 128; in every block some group is named by exactly 128 rows and some expert by exactly 128.
All inputs are finite; a program needn't handle non-finite values. No bound on the sum of `page_len` on one device may be relied on, other than what follows from the above.
Results may differ from a plain program's by a relative error of at most 0.02.
Values may be sent and summed in bfloat16 or wider, within the bound.
A program may use at most 64 MiB of HBM per device.

v0:
```python
import functools
import math

import jax
import jax.numpy as jnp
from jax import lax
from jax.experimental import pallas as pl
from jax.experimental.pallas import tpu as pltpu
from jax.sharding import PartitionSpec as P

QH = 32
KVH = 4
HD = 128
GROUPS_ROW = 4


NEG_FILL = -1e30
EPSILON = 1e-06
KEY_BLOCK = 1024
FAR_RANK = 1073741824
MESH = pl.DeviceIdType.MESH


def joined(x, axis, join):
    gathered = jax.tree.map(
        lambda a, kind: lax.all_gather(a.astype(kind), axis),
        x,
        jax.tree.map(lambda a: jnp.bfloat16 if a.dtype == jnp.float32 else a.dtype, x),
    )

    def take(source):
        return jax.tree.map(
            lambda a, own: lax.dynamic_index_in_dim(a, source, 0, False).astype(own.dtype),
            gathered,
            x,
        )

    return lax.fori_loop(
        1, lax.axis_size(axis), lambda source, state: join(state, take(source)), take(0)
    )


def block_sizes(block_rows, group_total, experts_group):
    group_slots = min(block_rows, 3 * GROUPS_ROW * block_rows // (2 * group_total))
    return (group_slots, 2 * group_slots // experts_group)


def attend_block(fold_state, packed, key_rank, query_heads, row_ids, kv_heads):
    running_max, weight_sum, weighted = fold_state
    half_cols = packed.shape[1] // 2
    length = packed.shape[0]
    key_part = packed[:, :half_cols].reshape(length, kv_heads, half_cols // kv_heads)
    value_part = packed[:, half_cols:].reshape(length, kv_heads, half_cols // kv_heads)
    scores = jnp.einsum(
        "rkqd,lkd->rkql", query_heads, key_part, preferred_element_type=jnp.float32
    ) * (1.0 / math.sqrt(HD))
    allowed = (key_rank[None, :] <= row_ids[:, None])[:, None, None, :]
    masked = jnp.where(allowed, scores, NEG_FILL)
    new_max = jnp.maximum(running_max, jnp.max(masked, axis=3))
    factor = jnp.exp(running_max - new_max)
    exp_terms = jnp.where(allowed, jnp.exp(scores - new_max[..., None]), 0.0)
    weight_sum = weight_sum * factor + jnp.sum(exp_terms, axis=3)
    weighted = weighted * factor[..., None] + jnp.einsum(
        "rkql,lkd->rkqd",
        exp_terms.astype(jnp.bfloat16),
        value_part,
        preferred_element_type=jnp.float32,
    )
    return (new_max, weight_sum, weighted)


def join_parts(first_part, second_part):
    first_max, first_sum, first_weighted = first_part
    second_max, second_sum, second_weighted = second_part
    joint_max = jnp.maximum(first_max, second_max)
    first_factor = jnp.exp(first_max - joint_max)
    second_factor = jnp.exp(second_max - joint_max)
    joint_sum = first_sum * first_factor + second_sum * second_factor
    joint_weighted = (
        first_weighted * first_factor[..., None] + second_weighted * second_factor[..., None]
    )
    return (joint_max, joint_sum, joint_weighted)


def shards(
    queries,
    cache_keys,
    cache_values,
    page_len,
    new_keys,
    new_values,
    out_proj,
    residual,
    norm_gain,
    gate_up,
    w_down,
    expert_ids,
    gates,
):
    query_rows = queries.shape[0]
    heads_here = queries.shape[1] // HD
    group_width = QH // KVH
    kv_heads = max(1, heads_here // group_width)
    per_kv = heads_here // kv_heads
    kv_first = lax.axis_index("hd") * heads_here // group_width

    def kv_columns(source):
        return lax.dynamic_slice_in_dim(source, kv_first * HD, kv_heads * HD, 1)

    local_keys = jnp.concatenate([kv_columns(cache_keys), kv_columns(new_keys)], axis=0)
    local_values = jnp.concatenate([kv_columns(cache_values), kv_columns(new_values)], axis=0)
    packed_local = jnp.concatenate([local_keys, local_values], axis=1)
    cache_rows = cache_keys.shape[0]
    new_rows = new_keys.shape[0]
    cache_rank = jnp.where(
        jnp.arange(cache_rows, dtype=jnp.int32) < page_len[0], -1, FAR_RANK
    ).astype(jnp.int32)
    new_block = lax.axis_index("ep") * lax.axis_size("sub") + lax.axis_index("sub")
    new_rank = new_block * new_rows + jnp.arange(new_rows, dtype=jnp.int32)
    rank_local = jnp.concatenate([cache_rank, new_rank], axis=0)
    row_ids = lax.axis_index("ep") * query_rows + jnp.arange(query_rows, dtype=jnp.int32)
    query_heads = queries.reshape(query_rows, kv_heads, per_kv, HD)

    def fold_keys(fold_state, piece_data):
        packed, key_rank = piece_data
        length = packed.shape[0]
        if length > KEY_BLOCK and length % KEY_BLOCK == 0:
            block_count = length // KEY_BLOCK

            def scan_step(inner_state, block_data):
                return (
                    attend_block(
                        inner_state, block_data[0], block_data[1], query_heads, row_ids, kv_heads
                    ),
                    None,
                )

            fold_state, _ = lax.scan(
                scan_step,
                fold_state,
                (
                    packed.reshape(block_count, KEY_BLOCK, packed.shape[1]),
                    key_rank.reshape(block_count, KEY_BLOCK),
                ),
            )
            return fold_state
        return attend_block(fold_state, packed, key_rank, query_heads, row_ids, kv_heads)

    start_state = (
        jnp.full((query_rows, kv_heads, per_kv), NEG_FILL, jnp.float32),
        jnp.zeros((query_rows, kv_heads, per_kv), jnp.float32),
        jnp.zeros((query_rows, kv_heads, per_kv, HD), jnp.float32),
    )
    fold_state = fold_keys(
        start_state,
        (
            lax.all_gather(packed_local, "ep", axis=0, tiled=True),
            lax.all_gather(rank_local, "ep", axis=0, tiled=True),
        ),
    )
    running_max, weight_sum, weighted = joined(fold_state, "sub", join_parts)
    attended = (
        (weighted / weight_sum[..., None]).reshape(query_rows, heads_here * HD).astype(jnp.bfloat16)
    )
    projected = lax.psum_scatter(
        jnp.dot(attended, out_proj, preferred_element_type=jnp.float32).astype(jnp.bfloat16),
        "hd",
        scatter_dimension=0,
        tiled=True,
    ).astype(jnp.float32)
    hidden_half = (residual.astype(jnp.float32) + projected).astype(jnp.bfloat16)
    widened = hidden_half.astype(jnp.float32)
    features = norm_gain.shape[0]
    half_width = hidden_half.shape[1]
    square_sum = lax.psum(jnp.sum(widened * widened, axis=1), "sub")
    gain_half = lax.dynamic_slice_in_dim(
        norm_gain, lax.axis_index("sub") * half_width, half_width, 0
    )
    normed = (
        widened
        * lax.rsqrt(square_sum[:, None] / features + EPSILON)
        * gain_half.astype(jnp.float32)
    ).astype(jnp.bfloat16)
    pair_weights = gate_up[0].reshape(-1, features)
    hidden_units = w_down.shape[1]
    group_total = lax.axis_size("ep")
    group_experts = lax.axis_size("hd")
    all_experts = group_total * group_experts
    block_rows = expert_ids.shape[0]
    group_slots, expert_slots = block_sizes(block_rows, group_total, group_experts)
    chosen = (
        expert_ids[:, :, None] == jnp.arange(all_experts, dtype=jnp.int32)[None, None, :]
    ).astype(jnp.int32)
    named_count = jnp.sum(chosen, axis=1)
    earlier = jnp.cumsum(named_count, axis=0) - named_count
    slot_index = jnp.sum(chosen * earlier[:, None, :], axis=2)
    position = expert_ids * expert_slots + slot_index
    slot_columns = jnp.arange(all_experts * expert_slots, dtype=jnp.int32)
    gate_table = jnp.sum(
        jnp.where(
            position[:, :, None] == slot_columns[None, None, :],
            gates.astype(jnp.float32)[:, :, None],
            0.0,
        ),
        axis=1,
    ).astype(jnp.bfloat16)
    placed = (gate_table != 0).astype(jnp.bfloat16)
    outgoing = jnp.einsum("rq,rd->qd", placed, normed, preferred_element_type=jnp.float32).astype(
        jnp.bfloat16
    )
    outgoing = outgoing.reshape(all_experts, expert_slots, normed.shape[1])
    arrived = lax.all_to_all(outgoing, ("ep", "hd"), split_axis=0, concat_axis=0, tiled=True)
    lead_shape = arrived.shape[:-1]
    rows_in = arrived.reshape(-1, arrived.shape[-1])
    rows_in = lax.all_gather(rows_in, "sub", axis=1, tiled=True)
    projected_pair = jnp.einsum(
        "rd,fd->rf", rows_in, pair_weights, preferred_element_type=jnp.float32
    )
    activation = (
        jax.nn.silu(projected_pair[:, :hidden_units]) * projected_pair[:, hidden_units:]
    ).astype(jnp.bfloat16)
    partial_out = jnp.dot(activation, w_down[0], preferred_element_type=jnp.float32)
    expert_out = lax.psum_scatter(
        partial_out.astype(jnp.bfloat16), "sub", scatter_dimension=1, tiled=True
    )
    results = expert_out.reshape(lead_shape + (expert_out.shape[1],))
    returned = lax.all_to_all(results, ("ep", "hd"), split_axis=0, concat_axis=0, tiled=True)
    mixture = jnp.dot(
        gate_table,
        returned.reshape(all_experts * expert_slots, half_width),
        preferred_element_type=jnp.float32,
    )
    return (widened + mixture).astype(jnp.bfloat16)


def slot_of(step, place, total):
    near = jnp.minimum(place, total - 1 - place)
    odd = place - (step + 1) // 2
    even = place + step // 2
    beside = jnp.where(step % 2 == 1, odd, even)
    beyond = jnp.where(place < total - 1 - place, step, total - 1 - step)
    return jnp.where(step <= 2 * near, beside, beyond)


(C_UP, C_DOWN, N_UP, X_UP, X_DOWN, W_SIDE, W_PART, Z_UP, Z_DOWN, P_SIDE) = range(10)
(C_IN, N_IN, X_IN, W_SIDE_IN, W_PART_IN, Z_IN, P_IN) = range(7)
SIB_COUNT = 17
LOG2_E = math.log2(math.e)


def layer_kernel(
    total, tiles,
    queries, cache_keys, cache_values, bias, new_keys, new_values, out_proj, residual, gain,
    gate_up, w_down, gate_dense,
    out,
    q_v, cbuf, nbuf, m_v, l_v, acc_v, att, proj_w, part_out, part_in, res_v, gain_v, hid, wgu,
    rows, results, chain_in,
    send_sem, recv_sem, load_sem, sib_send, sib_recv, proj_f, hid_out,
):
    e = lax.axis_index("ep")
    h = lax.axis_index("hd")
    s = lax.axis_index("sub")
    part = lax.axis_index("grp")
    last = total - 1
    heads = q_v.shape[0]
    page = new_keys.shape[0]
    page_c = cache_keys.shape[0]
    half = out.shape[2]
    own_rows = out.shape[1]
    features = 2 * half
    scale = LOG2_E / math.sqrt(HD)
    has_up = e < last
    has_down = e > 0

    def col(index, width):
        return pl.ds(pl.multiple_of(index * width, width), width)

    def local(index, src, dst):
        return pltpu.make_async_copy(src, dst, load_sem.at[index])

    mine = 2 * h + s
    loads = [
        local(0, cache_keys.at[:, col(mine, HD)], cbuf.at[e, s, pl.ds(0, page_c)]),
        local(1, cache_values.at[:, col(mine, HD)], cbuf.at[e, s, pl.ds(page_c, page_c)]),
        local(2, bias, cbuf.at[e, s, pl.ds(2 * page_c, 16)]),
        local(3, new_keys.at[:, col(mine, HD)], nbuf.at[e, s, pl.ds(0, page)]),
        local(4, new_values.at[:, col(mine, HD)], nbuf.at[e, s, pl.ds(page, page)]),
    ]
    q_loads = [
        local(16 + i, queries.at[:, col(s * heads + i, HD)], q_v.at[i]) for i in range(heads)
    ]
    w_loads = [
        local(5, out_proj, proj_w),
        local(6, residual, res_v),
        local(7, gain, gain_v),
        local(8, gate_dense.at[pl.ds(pl.multiple_of(s * own_rows, own_rows), own_rows)],
              rows.at[e, :, pl.ds(features, 128)]),
        local(9, gate_up.at[0], wgu.at[h, pl.ds(0, 2), s]),
        local(10, w_down.at[0], wgu.at[h, 2, s]),
    ]
    for copy in loads + q_loads + w_loads:
        copy.start()

    barrier = pltpu.get_barrier_semaphore()
    pl.semaphore_signal(barrier, inc=1, device_id={"sub": 1 - s}, device_id_type=MESH)
    pl.semaphore_signal(barrier, inc=1, device_id={"hd": 1 - h}, device_id_type=MESH)
    pl.semaphore_signal(barrier, inc=1, device_id={"grp": 1 - part}, device_id_type=MESH)

    @pl.when(has_up)
    def _():
        pl.semaphore_signal(barrier, inc=1, device_id={"ep": e + 1}, device_id_type=MESH)

    @pl.when(has_down)
    def _():
        pl.semaphore_signal(barrier, inc=1, device_id={"ep": e - 1}, device_id_type=MESH)

    pl.semaphore_wait(barrier, 3 + has_up.astype(jnp.int32) + has_down.astype(jnp.int32))

    def sibling(index, src, dst):
        return pltpu.make_async_remote_copy(
            src_ref=src, dst_ref=dst, send_sem=sib_send.at[index], recv_sem=sib_recv.at[index],
            device_id={"sub": 1 - s}, device_id_type=MESH)

    def remote(kind, index, arrival, slot, src, dst, where):
        return pltpu.make_async_remote_copy(
            src_ref=src, dst_ref=dst, send_sem=send_sem.at[kind, index],
            recv_sem=recv_sem.at[arrival, slot], device_id=where, device_id_type=MESH)

    theirs = 2 * h + 1 - s
    kv_sib = [
        sibling(0, cache_keys.at[:, col(theirs, HD)], cbuf.at[e, s, pl.ds(0, page_c)]),
        sibling(1, cache_values.at[:, col(theirs, HD)], cbuf.at[e, s, pl.ds(page_c, page_c)]),
        sibling(2, bias, cbuf.at[e, s, pl.ds(2 * page_c, 16)]),
        sibling(3, new_keys.at[:, col(theirs, HD)], nbuf.at[e, s, pl.ds(0, page)]),
        sibling(4, new_values.at[:, col(theirs, HD)], nbuf.at[e, s, pl.ds(page, page)]),
    ]
    w_sib = [
        sibling(5, gate_up.at[0], wgu.at[h, pl.ds(0, 2), s]),
        sibling(6, w_down.at[0], wgu.at[h, 2, s]),
    ]
    for copy in kv_sib:
        copy.start()

    cut = wgu.shape[3] // 2

    def cut_rows(which):
        return pl.ds(pl.multiple_of(which * cut, cut), cut)

    def w_side(piece):
        src = (w_down.at[0, cut_rows(part)] if piece == 2
               else gate_up.at[0, piece, cut_rows(part)])
        return remote(W_SIDE, piece, W_SIDE_IN, piece, src,
                      wgu.at[h, piece, s, cut_rows(part)], {"hd": 1 - h})

    def w_part(piece):
        block_ref = wgu.at[1 - h, piece, s, cut_rows(part)]
        return remote(W_PART, piece, W_PART_IN, piece, block_ref, block_ref, {"grp": 1 - part})

    def w_near(piece, which):
        block_ref = wgu.at[1 - h, piece, s, cut_rows(jnp.where(which == 0, part, 1 - part))]
        return sibling(10 + 2 * piece + which, block_ref, block_ref)

    def w_from_side(piece):
        block_ref = wgu.at[1 - h, piece, s, cut_rows(part)]
        remote(W_SIDE, piece, W_SIDE_IN, piece, block_ref, block_ref, {"hd": 1 - h}).wait_recv()
        w_part(piece).start()
        w_near(piece, 0).start()

    def w_from_part(piece):
        w_part(piece).wait_recv()
        w_near(piece, 1).start()

    for piece in range(3):
        w_side(piece).start()

    def c_up(i):
        return remote(C_UP, i, C_IN, i, cbuf.at[i], cbuf.at[i], {"ep": e + 1})

    def c_down(i):
        return remote(C_DOWN, i, C_IN, i, cbuf.at[i], cbuf.at[i], {"ep": e - 1})

    def n_up(i):
        return remote(N_UP, i, N_IN, i, nbuf.at[i], nbuf.at[i], {"ep": e + 1})

    for copy in loads:
        copy.wait()
    for copy in kv_sib:
        copy.wait_recv()

    @pl.when(has_up)
    def _():
        n_up(e).start()
        c_up(e).start()

    @pl.when(has_down)
    def _():
        c_down(e).start()

    for copy in w_sib:
        copy.start()
    for copy in q_loads:
        copy.wait()

    def parts_of(buf, index, size):
        return (buf[index, :, 0:size, :].reshape(2 * size, HD),
                buf[index, :, size:2 * size, :].reshape(2 * size, HD))

    def attend(index, with_cache, with_new, causal, first=False):
        pieces = []
        if with_cache:
            pieces.append(parts_of(cbuf, index, page_c))
            line = jnp.concatenate(
                [cbuf[index, 0, 2 * page_c:2 * page_c + 16, :],
                 cbuf[index, 1, 2 * page_c:2 * page_c + 16, :]], axis=1)[0:1].astype(jnp.float32)
        if with_new:
            pieces.append(parts_of(nbuf, index, page))

        def one_head(i, carry):
            query = q_v[i]
            scores = []
            for place, (key_part, _) in enumerate(pieces):
                one = lax.dot_general(
                    query, key_part, (((1,), (1,)), ((), ())), preferred_element_type=jnp.float32)
                if with_cache and place == 0:
                    one = one + line
                elif causal:
                    r = lax.broadcasted_iota(jnp.int32, one.shape, 0)
                    c = lax.broadcasted_iota(jnp.int32, one.shape, 1)
                    one = jnp.where(c <= r, one, NEG_FILL)
                scores.append(one)
            top = jnp.max(functools.reduce(
                jnp.maximum, [one[:, j:j + HD] for one in scores for j in range(0, one.shape[1], HD)]),
                axis=1, keepdims=True)
            if first:
                new = jnp.broadcast_to(top, m_v.shape[1:])
            else:
                old = m_v[i]
                new = jnp.maximum(old, top)
                factor = jnp.exp2((old - new) * scale)
            new_col = new[:, 0:1]
            weighted = None
            lane_sum = None
            for one, (_, value_part) in zip(scores, pieces):
                p = jnp.exp2((one - new_col) * scale)
                term = jnp.dot(p.astype(jnp.bfloat16), value_part, preferred_element_type=jnp.float32)
                weighted = term if weighted is None else weighted + term
                for j in range(0, p.shape[1], HD):
                    piece_sum = p[:, j:j + HD]
                    lane_sum = piece_sum if lane_sum is None else lane_sum + piece_sum
            m_v[i] = new
            if first:
                l_v[i] = lane_sum
                acc_v[i] = weighted
            else:
                l_v[i] = l_v[i] * factor + lane_sum
                acc_v[i] = acc_v[i] * factor + weighted
            return carry

        lax.fori_loop(0, heads, one_head, 0, unroll=2)

    attend(e, True, True, True, True)

    def kv_step(t, carry):
        i = slot_of(t, e, total)
        below = i < e

        @pl.when(below)
        def _():
            n_up(i).wait_recv()
        c_up(i).wait_recv()

        @pl.when(jnp.logical_and(below, has_up))
        def _():
            n_up(i).start()
            c_up(i).start()

        @pl.when(jnp.logical_and(jnp.logical_not(below), has_down))
        def _():
            c_down(i).start()

        @pl.when(below)
        def _():
            attend(i, True, True, False)

        @pl.when(jnp.logical_not(below))
        def _():
            attend(i, True, False, False)

        @pl.when(t == 1)
        def _():
            w_from_side(0)

        @pl.when(t == 2)
        def _():
            w_from_side(1)

        @pl.when(t == 3)
        def _():
            w_from_part(0)
        return carry

    lax.fori_loop(1, total, kv_step, 0)

    def finish_head(i, carry):
        att[s, :, col(i, HD)] = (
            acc_v[i] / jnp.sum(l_v[i], axis=1, keepdims=True)).astype(jnp.bfloat16)
        return carry

    lax.fori_loop(0, heads, finish_head, 0)
    block = 2 * own_rows

    def att_rows(which):
        return att.at[s, pl.ds(pl.multiple_of(which * block, block), block)]

    att_sib = sibling(7, att_rows(1 - h), att_rows(1 - h))
    att_sib.start()
    att_own = sibling(9, att_rows(h), att_rows(h))
    att_own.start()
    for copy in w_loads[:3]:
        copy.wait()
    att_sib.wait_recv()

    width = half // tiles
    contract = att.shape[2]

    def project(first_row, j):
        a0 = att[0, pl.ds(pl.multiple_of(first_row, block), block), :]
        a1 = att[1, pl.ds(pl.multiple_of(first_row, block), block), :]
        return jnp.dot(a0, proj_w[0:contract, col(j, width)], preferred_element_type=jnp.float32) + jnp.dot(
            a1, proj_w[contract:2 * contract, col(j, width)], preferred_element_type=jnp.float32)

    def p_side(j):
        return remote(P_SIDE, j, P_IN, j, part_out.at[j], part_in.at[j], {"hd": 1 - h})

    def project_theirs(j, carry):
        part_out[j] = project((1 - h) * block, j).astype(jnp.bfloat16)
        p_side(j).start()
        return carry

    lax.fori_loop(0, tiles, project_theirs, 0)
    w_from_side(2)
    w_from_part(1)
    att_own.wait_recv()

    def project_keep(j, carry):
        proj_f[j] = project(h * block, j)
        return carry

    lax.fori_loop(0, tiles, project_keep, 0)

    def hidden_tile(j, carry):
        p_side(j).wait_recv()
        res_v[:, col(j, width)] = (
            res_v[:, col(j, width)].astype(jnp.float32)
            + (proj_f[j] + part_in[j].astype(jnp.float32))).astype(jnp.bfloat16)
        return carry

    lax.fori_loop(0, tiles, hidden_tile, 0)

    def my_rows(which):
        return pl.ds(pl.multiple_of(which * own_rows, own_rows), own_rows)

    hid_sib = sibling(8, res_v.at[my_rows(1 - s)], hid.at[s])
    hid_sib.start()
    w_from_part(2)
    hid[s] = res_v[my_rows(s), :]
    hid_sib.wait_recv()
    h0 = hid[0].astype(jnp.float32)
    h1 = hid[1].astype(jnp.float32)
    square = jnp.sum(h0 * h0, axis=1, keepdims=True) + jnp.sum(h1 * h1, axis=1, keepdims=True)
    inverse = lax.rsqrt(square / features + EPSILON)
    g = gain_v[...].astype(jnp.float32)
    rows[e, :, 0:half] = (h0 * inverse * g[0:1, 0:half]).astype(jnp.bfloat16)
    rows[e, :, half:features] = (h1 * inverse * g[0:1, half:features]).astype(jnp.bfloat16)
    for copy in w_loads[3:]:
        copy.wait()
    for copy in w_sib:
        copy.wait_recv()

    def x_up(i):
        return remote(X_UP, i, X_IN, i, rows.at[i], rows.at[i], {"ep": e + 1})

    def x_down(i):
        return remote(X_DOWN, i, X_IN, i, rows.at[i], rows.at[i], {"ep": e - 1})

    def z_up(i, c):
        place = i + c * (total + 1)
        return remote(Z_UP, place, Z_IN, place, results.at[i, c], chain_in.at[i, c], {"ep": e + 1})

    def z_down(i, c):
        slot = jnp.where(i == e - 1, total, i)
        return remote(Z_DOWN, i + c * (total + 1), Z_IN, slot + c * (total + 1),
                      results.at[i, c], chain_in.at[slot, c], {"ep": e - 1})

    @pl.when(has_up)
    def _():
        x_up(e).start()

    @pl.when(has_down)
    def _():
        x_down(e).start()

    for piece in range(2):
        for which in range(2):
            w_near(piece, which).wait_recv()

    units = 2 * wgu.shape[3]
    dims = (((1,), (1,)), ((), ()))
    down_width = features // 4

    def arrive(step):
        n = slot_of(step, e, total)
        below = n < e
        x_up(n).wait_recv()

        @pl.when(jnp.logical_and(below, has_up))
        def _():
            x_up(n).start()

        @pl.when(jnp.logical_and(jnp.logical_not(below), has_down))
        def _():
            x_down(n).start()

    middle = jnp.logical_and(has_up, has_down)

    def expert_step(t, carry):
        i = slot_of(t, e, total)
        gates_all = rows[i, :, features:features + 128].astype(jnp.float32)
        lane = lax.broadcasted_iota(jnp.int32, gates_all.shape, 1)
        x = rows[i, :, 0:features]
        activations = []
        for which in range(2):
            gate_part = lax.dot_general(
                x, wgu[which, 0].reshape(units, features), dims, preferred_element_type=jnp.float32)
            up_part = lax.dot_general(
                x, wgu[which, 1].reshape(units, features), dims, preferred_element_type=jnp.float32)
            activations.append(
                (gate_part / (1.0 + jnp.exp(-gate_part)) * up_part).astype(jnp.bfloat16))
        weight = [
            jnp.sum(jnp.where(lane == 2 * e + which, gates_all, 0.0), axis=1, keepdims=True)
            for which in range(2)
        ]
        @pl.when(t == 0)
        def _():
            for which in range(2):
                w_near(2, which).wait_recv()

        for c in range(2):
            for j in range(2):
                span = slice((2 * c + j) * down_width, (2 * c + j + 1) * down_width)
                mixed = None
                for which in range(2):
                    piece = weight[which] * jnp.dot(
                        activations[which], wgu[which, 2, :, :, span].reshape(units, down_width),
                        preferred_element_type=jnp.float32)
                    mixed = piece if mixed is None else mixed + piece
                results[i, c, :, j * down_width:(j + 1) * down_width] = mixed.astype(jnp.bfloat16)

            @pl.when(jnp.logical_and(i > e, jnp.logical_not(has_down)))
            def _():
                z_up(i, c).start()

            @pl.when(jnp.logical_and(i < e, jnp.logical_not(has_up)))
            def _():
                z_down(i, c).start()

        @pl.when(t < jnp.where(middle, 1, last))
        def _():
            arrive(t + 1)

        @pl.when(jnp.logical_and(middle, t < last - 1))
        def _():
            arrive(t + 2)
        return carry

    lax.fori_loop(0, total, expert_step, 0)

    def add_chain(i, c):
        z_up(i, c).wait_recv()
        results[i, c] = (
            results[i, c].astype(jnp.float32) + chain_in[i, c].astype(jnp.float32)
        ).astype(jnp.bfloat16)

    def pass_up(i):
        @pl.when(jnp.logical_and(i <= last, has_down))
        def _():
            for c in range(2):
                add_chain(i, c)
                z_up(i, c).start()

    def pass_down(i):
        @pl.when(jnp.logical_and(i >= 0, has_up))
        def _():
            for c in range(2):
                add_chain(i, c)
                z_down(i, c).start()

    low_side = e < total // 2
    for phase in range(2):
        def chain_step(j, carry):
            up_now = low_side if phase == 0 else jnp.logical_not(low_side)

            @pl.when(up_now)
            def _():
                pass_up(e + j)

            @pl.when(jnp.logical_not(up_now))
            def _():
                pass_down(e - j)
            return carry

        lax.fori_loop(1, total, chain_step, 0)

    for c in range(2):
        @pl.when(has_down)
        def _():
            z_up(e, c).wait_recv()

        @pl.when(has_up)
        def _():
            place = total + c * (total + 1)
            remote(Z_UP, place, Z_IN, place, chain_in.at[total, c], chain_in.at[total, c],
                   {"ep": e + 1}).wait_recv()

    def side_sum(c):
        value = results[e, c].astype(jnp.float32)
        up_value = chain_in[e, c].astype(jnp.float32)
        down_value = chain_in[total, c].astype(jnp.float32)
        value = value + jnp.where(has_down, up_value, 0.0)
        return value + jnp.where(has_up, down_value, 0.0)

    first_half = (hid[0].astype(jnp.float32) + side_sum(0)).astype(jnp.bfloat16)
    second_half = (hid[1].astype(jnp.float32) + side_sum(1)).astype(jnp.bfloat16)
    is_first = s == 0
    out[s] = jnp.where(is_first, first_half, second_half)
    hid_out[...] = jnp.where(is_first, second_half, first_half)
    out_sib = sibling(16, hid_out, out.at[s])
    out_sib.start()
    out_sib.wait_recv()

    for piece in range(3):
        w_side(piece).wait_send()
        w_part(piece).wait_send()
        w_near(piece, 0).wait_send()
        w_near(piece, 1).wait_send()
    for copy in kv_sib + w_sib + [att_sib, att_own, hid_sib, out_sib]:
        copy.wait_send()

    def drain_tile(j, carry):
        p_side(j).wait_send()
        return carry

    lax.fori_loop(0, tiles, drain_tile, 0)

    def drain(i, carry):
        @pl.when(jnp.logical_and(i <= e, has_up))
        def _():
            n_up(i).wait_send()
            c_up(i).wait_send()
            x_up(i).wait_send()

        @pl.when(jnp.logical_and(i >= e, has_down))
        def _():
            c_down(i).wait_send()
            x_down(i).wait_send()

        @pl.when(i > e)
        def _():
            z_up(i, 0).wait_send()
            z_up(i, 1).wait_send()

        @pl.when(i < e)
        def _():
            z_down(i, 0).wait_send()
            z_down(i, 1).wait_send()
        return carry

    lax.fori_loop(0, total, drain, 0)


def fused_shards(
    queries, cache_keys, cache_values, page_len, new_keys, new_values, out_proj, residual,
    norm_gain, gate_up, w_down, expert_ids, gates,
):
    total = lax.axis_size("ep")
    all_experts = total * lax.axis_size("hd")
    query_rows = queries.shape[0]
    heads = queries.shape[1] // HD // 2
    block_rows, half = residual.shape
    features = 2 * half
    own_rows = block_rows // 2
    page_c, page = cache_keys.shape[0], new_keys.shape[0]
    hidden = w_down.shape[1]
    tiles = 4
    slots = max(2 * (total + 1), tiles)
    seen = jnp.arange(page_c, dtype=jnp.int32)[None, :] < page_len[0]
    bias = jnp.broadcast_to(jnp.where(seen, 0.0, NEG_FILL).astype(jnp.bfloat16), (16, page_c))
    lanes = jnp.arange(128, dtype=jnp.int32)
    gate_dense = jnp.sum(
        jnp.where(
            expert_ids[:, :, None] == lanes[None, None, :],
            gates.astype(jnp.float32)[:, :, None],
            0.0,
        ),
        axis=1,
    ).astype(jnp.bfloat16)
    anywhere = pl.BlockSpec(memory_space=pl.ANY)
    bf, f32 = jnp.bfloat16, jnp.float32
    out = pl.pallas_call(
        functools.partial(layer_kernel, total, tiles),
        out_shape=jax.ShapeDtypeStruct((2, own_rows, half), bf),
        in_specs=[anywhere] * 12,
        out_specs=pl.BlockSpec(memory_space=pltpu.VMEM),
        scratch_shapes=[
            pltpu.VMEM((heads, query_rows, HD), bf),
            pltpu.VMEM((total, 2, 2 * page_c + 16, HD), bf),
            pltpu.VMEM((total, 2, 2 * page, HD), bf),
            pltpu.VMEM((heads, query_rows, HD), f32),
            pltpu.VMEM((heads, query_rows, HD), f32),
            pltpu.VMEM((heads, query_rows, HD), f32),
            pltpu.VMEM((2, query_rows, heads * HD), bf),
            pltpu.VMEM(out_proj.shape, bf),
            pltpu.VMEM((tiles, block_rows, half // tiles), bf),
            pltpu.VMEM((tiles, block_rows, half // tiles), bf),
            pltpu.VMEM((block_rows, half), bf),
            pltpu.VMEM((1, features), bf),
            pltpu.VMEM((2, own_rows, half), bf),
            pltpu.VMEM((2, 3, 2, hidden, features), bf),
            pltpu.VMEM((total, own_rows, features + 128), bf),
            pltpu.VMEM((total, 2, own_rows, half), bf),
            pltpu.VMEM((total + 1, 2, own_rows, half), bf),
            pltpu.SemaphoreType.DMA((10, slots)),
            pltpu.SemaphoreType.DMA((7, slots)),
            pltpu.SemaphoreType.DMA((16 + heads,)),
            pltpu.SemaphoreType.DMA((SIB_COUNT,)),
            pltpu.SemaphoreType.DMA((SIB_COUNT,)),
            pltpu.VMEM((tiles, block_rows, half // tiles), f32),
            pltpu.VMEM((own_rows, half), bf),
        ],
        compiler_params=pltpu.CompilerParams(
            collective_id=0, has_side_effects=True, vmem_limit_bytes=58 * 1024 * 1024
        ),
    )(queries, cache_keys, cache_values, bias, new_keys, new_values, out_proj, residual,
      norm_gain.reshape(1, features), gate_up, w_down, gate_dense)
    return out.reshape(block_rows, half)


def layer(*arguments):
    queries, page_rows, ids = arguments[0], arguments[4].shape[0], arguments[11]
    pair = lax.axis_size("ep") >= 4 and lax.axis_size("grp") == 2
    pair = pair and lax.axis_size("hd") == 2 and lax.axis_size("sub") == 2
    slots = block_sizes(ids.shape[0], lax.axis_size("ep"), lax.axis_size("hd"))[1]
    group_width = QH // KVH
    whole_heads = queries.shape[1] == 2 * group_width * HD
    whole_pages = page_rows == 128 and arguments[1].shape[0] == 128
    rows_fit = queries.shape[0] == 2 * page_rows and ids.shape[0] % 32 == 0
    if pair and slots == ids.shape[0] and whole_heads and whole_pages and rows_fit:
        return fused_shards(*arguments)
    return shards(*arguments)


def solution(mesh):
    return jax.shard_map(
        layer,
        mesh=mesh,
        in_specs=(
            P(("grp", "ep"), "hd"),
            P(("grp", "ep", "sub"), None),
            P(("grp", "ep", "sub"), None),
            P(("grp", "ep", "sub")),
            P(("grp", "ep", "sub"), None),
            P(("grp", "ep", "sub"), None),
            P("hd", "sub"),
            P(("grp", "ep", "hd"), "sub"),
            P(),
            P(("ep", "hd"), None, "sub", None),
            P(("ep", "hd"), "sub", None),
            P(("grp", "ep", "hd"), None),
            P(("grp", "ep", "hd"), None),
        ),
        out_specs=P(("grp", "ep", "hd"), "sub"),
        check_vma=False,
    )
```

profile of v0, /device:TPU:0, one launch (start us, length us, event | category | flops | bytes accessed | tf_op | source)
XLA Modules:
  0.0 96.5 jit_solution(6287853017132946472)
XLA Ops:
  0.7 0.6 broadcast_in_dim.31.bias
  1.3 1.3 %reshape.17.gain = bf16[1,2048]{1,0:T(2,128)(2,1)} reshape(bf16[2048]{0:T(1024)(128)(2,1)} %param.21) | data formatting | bytes 8192 | tf_op jit(solution)/shard_map/reshape | solution.py:844
  2.5 0.8 copy.16
  3.3 0.8 copy.17
  4.1 1.0 %select_reduce_fusion.gate_dense = bf16[128,128]{1,0:T(8,128)(2,1)} fusion(f32[128,8]{1,0:T(8,128)S(1)} %copy.17, s32[128,8]{1,0:T(8,128)S(1)} %copy.16), kind=kLoop, calls=%fused_computation | loop fusion | flops 376832 | bytes 40960 | tf_op jit(solution)/shard_map/reduce_sum | solution.py:799
  5.1 89.8 %shard_map.127 = bf16[2,64,1024]{2,1,0:T(8,128)(2,1)} custom-call(bf16[256,2048]{1,0:T(8,128)(2,1)} %queries.1, bf16[128,512]{1,0:T(8,128)(2,1)} %cache_keys.1, bf16[128,512]{1,0:T(8,128)(2,1)} %cache_values.1, bf16[16,128]{1,0:T(8,128)(2,1)} %broadcast_in_dim.31.bias, bf16[128,512]{1,0:T(8,128)(2,1)} %new_keys.1, bf16[128,512]{1,0:T(8,128)(2,1)} %new_values.1, ...), custom_call_target="tpu_custom_call" | custom-call | tf_op jit(solution)/shard_map/pallas_call | solution.py:809
  94.9 1.7 %copy.20 = bf16[128,1024]{1,0:T(8,128)(2,1)} copy(bf16[128,1024]{1,0:T(8,128)(2,1)} %bitcast.3) | data formatting | bytes 524288
  (1 shorter events, 0.0 us)
where the time goes:
time: 96.8 us; the launch traced here: 96.5 us
  Pallas kernels  89.8 us (93%)
  local copies, waits for them, and re-layouts  5.12 us (5%)
  other arithmetic  0.98 us (1%)
    pallas_call x1, Pallas kernels, fused_shards(): pl.pallas_call(functools.partial(layer_kernel, total, tiles), out_shape=j...  89.8 us
    unnamed x2, local copies, waits for them, and re-layouts  2.46 us

commit v1 on v0

--- a/solution.py
+++ b/solution.py
@@ -250,12 +250,12 @@
 
 def layer_kernel(
     total, tiles,
-    queries, cache_keys, cache_values, bias, new_keys, new_values, out_proj, residual, gain,
-    gate_up, w_down, gate_dense,
+    page_len, queries, cache_keys, cache_values, new_keys, new_values, out_proj, residual, gain_v,
+    gate_up, w_down, ids_t, gates_t,
     out,
-    q_v, cbuf, nbuf, m_v, l_v, acc_v, att, proj_w, part_out, part_in, res_v, gain_v, hid, wgu,
+    q_v, cbuf, nbuf, m_v, l_v, acc_v, att, proj_w, part_out, part_in, res_v, hid, wgu,
     rows, results, chain_in,
-    send_sem, recv_sem, load_sem, sib_send, sib_recv, proj_f, hid_out,
+    send_sem, recv_sem, load_sem, sib_send, sib_recv, proj_f, hid_out, gate_cols,
 ):
     e = lax.axis_index("ep")
     h = lax.axis_index("hd")
@@ -282,7 +282,6 @@
     loads = [
         local(0, cache_keys.at[:, col(mine, HD)], cbuf.at[e, s, pl.ds(0, page_c)]),
         local(1, cache_values.at[:, col(mine, HD)], cbuf.at[e, s, pl.ds(page_c, page_c)]),
-        local(2, bias, cbuf.at[e, s, pl.ds(2 * page_c, 16)]),
         local(3, new_keys.at[:, col(mine, HD)], nbuf.at[e, s, pl.ds(0, page)]),
         local(4, new_values.at[:, col(mine, HD)], nbuf.at[e, s, pl.ds(page, page)]),
     ]
@@ -292,15 +291,25 @@
     w_loads = [
         local(5, out_proj, proj_w),
         local(6, residual, res_v),
-        local(7, gain, gain_v),
-        local(8, gate_dense.at[pl.ds(pl.multiple_of(s * own_rows, own_rows), own_rows)],
-              rows.at[e, :, pl.ds(features, 128)]),
         local(9, gate_up.at[0], wgu.at[h, pl.ds(0, 2), s]),
         local(10, w_down.at[0], wgu.at[h, 2, s]),
     ]
     for copy in loads + q_loads + w_loads:
         copy.start()
 
+    experts = 2 * total
+    lane = lax.broadcasted_iota(jnp.int32, (8, HD), 1)
+    seen = jnp.where(lane < page_len[0], 0.0, NEG_FILL)
+    ids = ids_t[...]
+    gate_values = gates_t[...].astype(jnp.float32)
+    place = lax.broadcasted_iota(jnp.int32, (8, HD), 0)
+    by_expert = jnp.zeros((8, HD), jnp.float32)
+    for x in range(experts):
+        one_row = jnp.sum(jnp.where(ids == x, gate_values, 0.0), axis=0, keepdims=True)
+        by_expert = jnp.where(place == x, one_row, by_expert)
+    cbuf[e, s, 2 * page_c:2 * page_c + 16, :] = jnp.concatenate(
+        [seen, by_expert], axis=0).astype(jnp.bfloat16)
+
     barrier = pltpu.get_barrier_semaphore()
     pl.semaphore_signal(barrier, inc=1, device_id={"sub": 1 - s}, device_id_type=MESH)
     pl.semaphore_signal(barrier, inc=1, device_id={"hd": 1 - h}, device_id_type=MESH)
@@ -330,7 +339,7 @@
     kv_sib = [
         sibling(0, cache_keys.at[:, col(theirs, HD)], cbuf.at[e, s, pl.ds(0, page_c)]),
         sibling(1, cache_values.at[:, col(theirs, HD)], cbuf.at[e, s, pl.ds(page_c, page_c)]),
-        sibling(2, bias, cbuf.at[e, s, pl.ds(2 * page_c, 16)]),
+        sibling(2, cbuf.at[e, s, pl.ds(2 * page_c, 16)], cbuf.at[e, s, pl.ds(2 * page_c, 16)]),
         sibling(3, new_keys.at[:, col(theirs, HD)], nbuf.at[e, s, pl.ds(0, page)]),
         sibling(4, new_values.at[:, col(theirs, HD)], nbuf.at[e, s, pl.ds(page, page)]),
     ]
@@ -490,16 +499,18 @@
         def _():
             w_from_side(0)
 
-        @pl.when(t == 2)
+        @pl.when(t == 3)
         def _():
             w_from_side(1)
-
-        @pl.when(t == 3)
-        def _():
-            w_from_part(0)
         return carry
 
     lax.fori_loop(1, total, kv_step, 0)
+
+    def gate_step(i, carry):
+        flat = cbuf[i, 0, 2 * page_c:2 * page_c + 16, :].astype(jnp.float32)[8:16]
+        gate_cols[i] = jnp.concatenate(
+            [flat, jnp.zeros((HD - 8, HD), jnp.float32)], axis=0).T
+        return carry
 
     def finish_head(i, carry):
         att[s, :, col(i, HD)] = (
@@ -516,7 +527,7 @@
     att_sib.start()
     att_own = sibling(9, att_rows(h), att_rows(h))
     att_own.start()
-    for copy in w_loads[:3]:
+    for copy in w_loads[:2]:
         copy.wait()
     att_sib.wait_recv()
 
@@ -538,8 +549,7 @@
         return carry
 
     lax.fori_loop(0, tiles, project_theirs, 0)
-    w_from_side(2)
-    w_from_part(1)
+    w_from_part(0)
     att_own.wait_recv()
 
     def project_keep(j, carry):
@@ -547,6 +557,8 @@
         return carry
 
     lax.fori_loop(0, tiles, project_keep, 0)
+    lax.fori_loop(0, total, gate_step, 0)
+    w_from_side(2)
 
     def hidden_tile(j, carry):
         p_side(j).wait_recv()
@@ -562,17 +574,16 @@
 
     hid_sib = sibling(8, res_v.at[my_rows(1 - s)], hid.at[s])
     hid_sib.start()
-    w_from_part(2)
     hid[s] = res_v[my_rows(s), :]
     hid_sib.wait_recv()
     h0 = hid[0].astype(jnp.float32)
     h1 = hid[1].astype(jnp.float32)
     square = jnp.sum(h0 * h0, axis=1, keepdims=True) + jnp.sum(h1 * h1, axis=1, keepdims=True)
     inverse = lax.rsqrt(square / features + EPSILON)
-    g = gain_v[...].astype(jnp.float32)
+    g = gain_v[...].astype(jnp.float32).reshape(1, features)
     rows[e, :, 0:half] = (h0 * inverse * g[0:1, 0:half]).astype(jnp.bfloat16)
     rows[e, :, half:features] = (h1 * inverse * g[0:1, half:features]).astype(jnp.bfloat16)
-    for copy in w_loads[3:]:
+    for copy in w_loads[2:]:
         copy.wait()
     for copy in w_sib:
         copy.wait_recv()
@@ -600,6 +611,7 @@
     def _():
         x_down(e).start()
 
+    w_from_part(1)
     for piece in range(2):
         for which in range(2):
             w_near(piece, which).wait_recv()
@@ -625,9 +637,7 @@
 
     def expert_step(t, carry):
         i = slot_of(t, e, total)
-        gates_all = rows[i, :, features:features + 128].astype(jnp.float32)
-        lane = lax.broadcasted_iota(jnp.int32, gates_all.shape, 1)
-        x = rows[i, :, 0:features]
+        x = rows[i]
         activations = []
         for which in range(2):
             gate_part = lax.dot_general(
@@ -636,12 +646,15 @@
                 x, wgu[which, 1].reshape(units, features), dims, preferred_element_type=jnp.float32)
             activations.append(
                 (gate_part / (1.0 + jnp.exp(-gate_part)) * up_part).astype(jnp.bfloat16))
+        gates_all = gate_cols[i, my_rows(s), :]
+        gate_lane = lax.broadcasted_iota(jnp.int32, gates_all.shape, 1)
         weight = [
-            jnp.sum(jnp.where(lane == 2 * e + which, gates_all, 0.0), axis=1, keepdims=True)
+            jnp.sum(jnp.where(gate_lane == 2 * e + which, gates_all, 0.0), axis=1, keepdims=True)
             for which in range(2)
         ]
         @pl.when(t == 0)
         def _():
+            w_from_part(2)
             for which in range(2):
                 w_near(2, which).wait_recv()
 
@@ -793,23 +806,14 @@
     hidden = w_down.shape[1]
     tiles = 4
     slots = max(2 * (total + 1), tiles)
-    seen = jnp.arange(page_c, dtype=jnp.int32)[None, :] < page_len[0]
-    bias = jnp.broadcast_to(jnp.where(seen, 0.0, NEG_FILL).astype(jnp.bfloat16), (16, page_c))
-    lanes = jnp.arange(128, dtype=jnp.int32)
-    gate_dense = jnp.sum(
-        jnp.where(
-            expert_ids[:, :, None] == lanes[None, None, :],
-            gates.astype(jnp.float32)[:, :, None],
-            0.0,
-        ),
-        axis=1,
-    ).astype(jnp.bfloat16)
     anywhere = pl.BlockSpec(memory_space=pl.ANY)
+    vmem = pl.BlockSpec(memory_space=pltpu.VMEM)
     bf, f32 = jnp.bfloat16, jnp.float32
     out = pl.pallas_call(
         functools.partial(layer_kernel, total, tiles),
         out_shape=jax.ShapeDtypeStruct((2, own_rows, half), bf),
-        in_specs=[anywhere] * 12,
+        in_specs=[pl.BlockSpec(memory_space=pltpu.SMEM)] + [anywhere] * 7 + [vmem] + [anywhere] * 2
+        + [vmem] * 2,
         out_specs=pl.BlockSpec(memory_space=pltpu.VMEM),
         scratch_shapes=[
             pltpu.VMEM((heads, query_rows, HD), bf),
@@ -823,10 +827,9 @@
             pltpu.VMEM((tiles, block_rows, half // tiles), bf),
             pltpu.VMEM((tiles, block_rows, half // tiles), bf),
             pltpu.VMEM((block_rows, half), bf),
-            pltpu.VMEM((1, features), bf),
             pltpu.VMEM((2, own_rows, half), bf),
             pltpu.VMEM((2, 3, 2, hidden, features), bf),
-            pltpu.VMEM((total, own_rows, features + 128), bf),
+            pltpu.VMEM((total, own_rows, features), bf),
             pltpu.VMEM((total, 2, own_rows, half), bf),
             pltpu.VMEM((total + 1, 2, own_rows, half), bf),
             pltpu.SemaphoreType.DMA((10, slots)),
@@ -836,12 +839,13 @@
             pltpu.SemaphoreType.DMA((SIB_COUNT,)),
             pltpu.VMEM((tiles, block_rows, half // tiles), f32),
             pltpu.VMEM((own_rows, half), bf),
+            pltpu.VMEM((total, 2 * own_rows, 128), f32),
         ],
         compiler_params=pltpu.CompilerParams(
             collective_id=0, has_side_effects=True, vmem_limit_bytes=58 * 1024 * 1024
         ),
-    )(queries, cache_keys, cache_values, bias, new_keys, new_values, out_proj, residual,
-      norm_gain.reshape(1, features), gate_up, w_down, gate_dense)
+    )(page_len, queries, cache_keys, cache_values, new_keys, new_values, out_proj, residual,
+      norm_gain, gate_up, w_down, expert_ids.T, gates.T)
     return out.reshape(block_rows, half)
 
 
@@ -853,7 +857,8 @@
     group_width = QH // KVH
     whole_heads = queries.shape[1] == 2 * group_width * HD
     whole_pages = page_rows == 128 and arguments[1].shape[0] == 128
-    rows_fit = queries.shape[0] == 2 * page_rows and ids.shape[0] % 32 == 0
+    rows_fit = queries.shape[0] == 2 * page_rows and ids.shape == (128, 8)
+    rows_fit = rows_fit and lax.axis_size("ep") == 4
     if pair and slots == ids.shape[0] and whole_heads and whole_pages and rows_fit:
         return fused_shards(*arguments)
     return shards(*arguments)

time: 96.8 us -> 91.7 us (0.947)
  local copies, waits for them, and re-layouts: 5.12 us -> 1.67 us
  other arithmetic: 0.98 us -> 0 us
    reshape x1 -> x0, local copies, waits for them, and re-layouts: 1.28 us -> none  [fused_shards(): norm_gain.reshape(1, features)]
    reduce_sum x1 -> x0, other arithmetic: 0.98 us -> none  [fused_shards(): jnp.sum(jnp.where(expert_ids[:, :, None] == lanes[None, None, :], gates.a...]
    unnamed x2 -> x1, local copies, waits for them, and re-layouts: 2.46 us -> 1.67 us
where the time goes in v1:
time: 91.7 us; the launch traced here: 91.4 us
  Pallas kernels  89.1 us (97%)
  local copies, waits for them, and re-layouts  1.67 us (2%)
    pallas_call x1, Pallas kernels, fused_shards(): pl.pallas_call(functools.partial(layer_kernel, total, tiles), out_shape=j...  89.1 us

profile of v1, /device:TPU:0, one launch (start us, length us, event | category | flops | bytes accessed | tf_op | source)
XLA Modules:
  0.0 91.4 jit_solution(13693019862177305945)
XLA Ops:
  0.7 89.1 %shard_map.127 = bf16[2,64,1024]{2,1,0:T(8,128)(2,1)} custom-call(s32[1]{0:T(128)S(6)} %copy.15.page_len, bf16[256,2048]{1,0:T(8,128)(2,1)} %queries.1, bf16[128,512]{1,0:T(8,128)(2,1)} %cache_keys.1, bf16[128,512]{1,0:T(8,128)(2,1)} %cache_values.1, bf16[128,512]{1,0:T(8,128)(2,1)} %new_keys.1, bf16[128,512]{1,0:T(8,128)(2,1)} %new_values.1, ...), custom_call_target="tpu_custom_call" | custom-call | tf_op jit(solution)/shard_map/pallas_call | solution.py:812
  89.8 1.7 %copy.16 = bf16[128,1024]{1,0:T(8,128)(2,1)} copy(bf16[128,1024]{1,0:T(8,128)(2,1)} %bitcast.3) | data formatting | bytes 524288

commit v2 on v1

--- a/solution.py
+++ b/solution.py
@@ -244,8 +244,18 @@
 
 (C_UP, C_DOWN, N_UP, X_UP, X_DOWN, W_SIDE, W_PART, Z_UP, Z_DOWN, P_SIDE) = range(10)
 (C_IN, N_IN, X_IN, W_SIDE_IN, W_PART_IN, Z_IN, P_IN) = range(7)
-SIB_COUNT = 17
+SIB_COUNT = 25
+W_PIECES = 6
+X_CUTS = 2
+Z_CUTS = 4
 LOG2_E = math.log2(math.e)
+
+
+def semaphore_places(total, tiles):
+    sent = (total, total, total, X_CUTS * total, X_CUTS * total, W_PIECES, W_PIECES,
+            Z_CUTS * total, Z_CUTS * total, tiles)
+    arrived = (total, total, X_CUTS * total, W_PIECES, W_PIECES, Z_CUTS * (total + 1), tiles)
+    return [[sum(sizes[:i]) for i in range(len(sizes) + 1)] for sizes in (sent, arrived)]
 
 
 def layer_kernel(
@@ -255,7 +265,7 @@
     out,
     q_v, cbuf, nbuf, m_v, l_v, acc_v, att, proj_w, part_out, part_in, res_v, hid, wgu,
     rows, results, chain_in,
-    send_sem, recv_sem, load_sem, sib_send, sib_recv, proj_f, hid_out, gate_cols,
+    send_sem, recv_sem, load_sem, sib_send, sib_recv, proj_f, out_buf, gate_cols,
 ):
     e = lax.axis_index("ep")
     h = lax.axis_index("hd")
@@ -270,6 +280,7 @@
     features = 2 * half
     scale = LOG2_E / math.sqrt(HD)
     has_up = e < last
+    sent_at, arrived_at = semaphore_places(total, tiles)
     has_down = e > 0
 
     def col(index, width):
@@ -332,8 +343,8 @@
 
     def remote(kind, index, arrival, slot, src, dst, where):
         return pltpu.make_async_remote_copy(
-            src_ref=src, dst_ref=dst, send_sem=send_sem.at[kind, index],
-            recv_sem=recv_sem.at[arrival, slot], device_id=where, device_id_type=MESH)
+            src_ref=src, dst_ref=dst, send_sem=send_sem.at[sent_at[kind] + index],
+            recv_sem=recv_sem.at[arrived_at[arrival] + slot], device_id=where, device_id_type=MESH)
 
     theirs = 2 * h + 1 - s
     kv_sib = [
@@ -351,26 +362,31 @@
         copy.start()
 
     cut = wgu.shape[3] // 2
-
-    def cut_rows(which):
-        return pl.ds(pl.multiple_of(which * cut, cut), cut)
+    piece_rows = cut // 2
+
+    def cut_rows(which, piece):
+        return pl.ds(pl.multiple_of(which * cut + piece % 2 * piece_rows, piece_rows), piece_rows)
+
+    def w_block(piece, which):
+        return wgu.at[1 - h, piece // 2, s, cut_rows(which, piece)]
 
     def w_side(piece):
-        src = (w_down.at[0, cut_rows(part)] if piece == 2
-               else gate_up.at[0, piece, cut_rows(part)])
+        kind = piece // 2
+        src = (w_down.at[0, cut_rows(part, piece)] if kind == 2
+               else gate_up.at[0, kind, cut_rows(part, piece)])
         return remote(W_SIDE, piece, W_SIDE_IN, piece, src,
-                      wgu.at[h, piece, s, cut_rows(part)], {"hd": 1 - h})
+                      wgu.at[h, kind, s, cut_rows(part, piece)], {"hd": 1 - h})
 
     def w_part(piece):
-        block_ref = wgu.at[1 - h, piece, s, cut_rows(part)]
+        block_ref = w_block(piece, part)
         return remote(W_PART, piece, W_PART_IN, piece, block_ref, block_ref, {"grp": 1 - part})
 
     def w_near(piece, which):
-        block_ref = wgu.at[1 - h, piece, s, cut_rows(jnp.where(which == 0, part, 1 - part))]
-        return sibling(10 + 2 * piece + which, block_ref, block_ref)
+        block_ref = w_block(piece, jnp.where(which == 0, part, 1 - part))
+        return sibling(11 + 2 * piece + which, block_ref, block_ref)
 
     def w_from_side(piece):
-        block_ref = wgu.at[1 - h, piece, s, cut_rows(part)]
+        block_ref = w_block(piece, part)
         remote(W_SIDE, piece, W_SIDE_IN, piece, block_ref, block_ref, {"hd": 1 - h}).wait_recv()
         w_part(piece).start()
         w_near(piece, 0).start()
@@ -379,7 +395,7 @@
         w_part(piece).wait_recv()
         w_near(piece, 1).start()
 
-    for piece in range(3):
+    for piece in range(W_PIECES):
         w_side(piece).start()
 
     def c_up(i):
@@ -465,30 +481,64 @@
                 acc_v[i] = acc_v[i] * factor + weighted
             return carry
 
-        lax.fori_loop(0, heads, one_head, 0, unroll=2)
+        lax.fori_loop(0, heads, one_head, 0, unroll=8)
 
     attend(e, True, True, True, True)
+
+    middle = jnp.logical_and(has_up, has_down)
+    low_side = e < total // 2
+
+    def kv_arrive(t):
+        @pl.when(jnp.logical_not(middle))
+        def _():
+            i = slot_of(t, e, total)
+
+            @pl.when(i < e)
+            def _():
+                n_up(i).wait_recv()
+            c_up(i).wait_recv()
+
+        @pl.when(jnp.logical_and(middle, t == 1))
+        def _():
+            n_up(e - 1).wait_recv()
+            n_up(e - 1).start()
+            c_down(e + 1).wait_recv()
+            c_down(e + 1).start()
+            c_up(e - 1).wait_recv()
+            c_up(e - 1).start()
+
+        @pl.when(jnp.logical_and(jnp.logical_and(middle, low_side), t == 2))
+        def _():
+            c_down(last).wait_recv()
+            c_down(last).start()
+
+        @pl.when(jnp.logical_and(middle, jnp.logical_not(low_side)))
+        def _():
+            @pl.when(t == 2)
+            def _():
+                n_up(0).wait_recv()
+                n_up(0).start()
+
+            @pl.when(t == 3)
+            def _():
+                c_up(0).wait_recv()
+                c_up(0).start()
 
     def kv_step(t, carry):
         i = slot_of(t, e, total)
         below = i < e
+        kv_arrive(t)
+
+        @pl.when(t == 1)
+        def _():
+            w_from_side(0)
+
+        @pl.when(jnp.logical_and(t == 3, jnp.logical_not(middle)))
+        def _():
+            w_from_side(3)
 
         @pl.when(below)
         def _():
-            n_up(i).wait_recv()
-        c_up(i).wait_recv()
-
-        @pl.when(jnp.logical_and(below, has_up))
-        def _():
-            n_up(i).start()
-            c_up(i).start()
-
-        @pl.when(jnp.logical_and(jnp.logical_not(below), has_down))
-        def _():
-            c_down(i).start()
-
-        @pl.when(below)
-        def _():
             attend(i, True, True, False)
 
         @pl.when(jnp.logical_not(below))
@@ -497,11 +547,18 @@
 
         @pl.when(t == 1)
         def _():
-            w_from_side(0)
+            w_from_side(1)
+
+        @pl.when(t == 2)
+        def _():
+            w_from_side(2)
 
         @pl.when(t == 3)
         def _():
-            w_from_side(1)
+            @pl.when(middle)
+            def _():
+                w_from_side(3)
+            w_from_part(0)
         return carry
 
     lax.fori_loop(1, total, kv_step, 0)
@@ -532,111 +589,163 @@
     att_sib.wait_recv()
 
     width = half // tiles
+    side_width = half // (tiles // X_CUTS)
     contract = att.shape[2]
 
-    def project(first_row, j):
-        a0 = att[0, pl.ds(pl.multiple_of(first_row, block), block), :]
-        a1 = att[1, pl.ds(pl.multiple_of(first_row, block), block), :]
-        return jnp.dot(a0, proj_w[0:contract, col(j, width)], preferred_element_type=jnp.float32) + jnp.dot(
-            a1, proj_w[contract:2 * contract, col(j, width)], preferred_element_type=jnp.float32)
+    x_rows = own_rows // X_CUTS
+
+    def x_cut(i, k):
+        return rows.at[i, pl.ds(k * x_rows, x_rows)]
+
+    def x_up(i, k):
+        return remote(X_UP, X_CUTS * i + k, X_IN, X_CUTS * i + k, x_cut(i, k), x_cut(i, k),
+                      {"ep": e + 1})
+
+    def x_down(i, k):
+        return remote(X_DOWN, X_CUTS * i + k, X_IN, X_CUTS * i + k, x_cut(i, k), x_cut(i, k),
+                      {"ep": e - 1})
+
+    def z_up(i, c):
+        place = i + c * (total + 1)
+        return remote(Z_UP, i + c * total, Z_IN, place, results.at[i, c], chain_in.at[i, c], {"ep": e + 1})
+
+    def z_down(i, c):
+        slot = jnp.where(i == e - 1, total, i)
+        return remote(Z_DOWN, i + c * total, Z_IN, slot + c * (total + 1),
+                      results.at[i, c], chain_in.at[slot, c], {"ep": e - 1})
+
+    def project(a0, a1, j, size):
+        return jnp.dot(
+            a0, proj_w[0:contract, col(j, size)], preferred_element_type=jnp.float32
+        ) + jnp.dot(
+            a1, proj_w[contract:2 * contract, col(j, size)], preferred_element_type=jnp.float32)
 
     def p_side(j):
         return remote(P_SIDE, j, P_IN, j, part_out.at[j], part_in.at[j], {"hd": 1 - h})
 
     def project_theirs(j, carry):
-        part_out[j] = project((1 - h) * block, j).astype(jnp.bfloat16)
+        first = (1 - h) * block + j // (tiles // X_CUTS) * x_rows
+        a0, a1 = [
+            jnp.concatenate([
+                att[which, pl.ds(pl.multiple_of(first + u * own_rows, x_rows), x_rows), :]
+                for u in range(2)], axis=0)
+            for which in range(2)]
+        part_out[j] = project(a0, a1, j % (tiles // X_CUTS), side_width).astype(jnp.bfloat16)
         p_side(j).start()
         return carry
 
     lax.fori_loop(0, tiles, project_theirs, 0)
-    w_from_part(0)
+    w_from_side(4)
+    w_from_part(1)
     att_own.wait_recv()
 
     def project_keep(j, carry):
-        proj_f[j] = project(h * block, j)
+        own = pl.ds(pl.multiple_of(h * block, block), block)
+        proj_f[:, col(j, width)] = project(att[0, own, :], att[1, own, :], j, width)
         return carry
 
     lax.fori_loop(0, tiles, project_keep, 0)
     lax.fori_loop(0, total, gate_step, 0)
-    w_from_side(2)
-
-    def hidden_tile(j, carry):
-        p_side(j).wait_recv()
-        res_v[:, col(j, width)] = (
-            res_v[:, col(j, width)].astype(jnp.float32)
-            + (proj_f[j] + part_in[j].astype(jnp.float32))).astype(jnp.bfloat16)
-        return carry
-
-    lax.fori_loop(0, tiles, hidden_tile, 0)
+    w_from_side(5)
+    w_from_part(2)
+    w_from_part(3)
 
     def my_rows(which):
         return pl.ds(pl.multiple_of(which * own_rows, own_rows), own_rows)
 
-    hid_sib = sibling(8, res_v.at[my_rows(1 - s)], hid.at[s])
-    hid_sib.start()
-    hid[s] = res_v[my_rows(s), :]
-    hid_sib.wait_recv()
-    h0 = hid[0].astype(jnp.float32)
-    h1 = hid[1].astype(jnp.float32)
-    square = jnp.sum(h0 * h0, axis=1, keepdims=True) + jnp.sum(h1 * h1, axis=1, keepdims=True)
-    inverse = lax.rsqrt(square / features + EPSILON)
-    g = gain_v[...].astype(jnp.float32).reshape(1, features)
-    rows[e, :, 0:half] = (h0 * inverse * g[0:1, 0:half]).astype(jnp.bfloat16)
-    rows[e, :, half:features] = (h1 * inverse * g[0:1, half:features]).astype(jnp.bfloat16)
+    def my_cut(which, k):
+        return pl.ds(pl.multiple_of(which * own_rows + k * x_rows, x_rows), x_rows)
+
+    def hid_sib(k):
+        return sibling(8 + 2 * k, res_v.at[my_cut(1 - s, k)], hid.at[s, pl.ds(k * x_rows, x_rows)])
+
     for copy in w_loads[2:]:
         copy.wait()
     for copy in w_sib:
         copy.wait_recv()
-
-    def x_up(i):
-        return remote(X_UP, i, X_IN, i, rows.at[i], rows.at[i], {"ep": e + 1})
-
-    def x_down(i):
-        return remote(X_DOWN, i, X_IN, i, rows.at[i], rows.at[i], {"ep": e - 1})
-
-    def z_up(i, c):
-        place = i + c * (total + 1)
-        return remote(Z_UP, place, Z_IN, place, results.at[i, c], chain_in.at[i, c], {"ep": e + 1})
-
-    def z_down(i, c):
-        slot = jnp.where(i == e - 1, total, i)
-        return remote(Z_DOWN, i + c * (total + 1), Z_IN, slot + c * (total + 1),
-                      results.at[i, c], chain_in.at[slot, c], {"ep": e - 1})
-
-    @pl.when(has_up)
-    def _():
-        x_up(e).start()
-
-    @pl.when(has_down)
-    def _():
-        x_down(e).start()
-
-    w_from_part(1)
-    for piece in range(2):
-        for which in range(2):
-            w_near(piece, which).wait_recv()
-
+    g = gain_v[...].astype(jnp.float32).reshape(1, features)
+    for k in range(X_CUTS):
+        for j in range(tiles // X_CUTS):
+            place = k * (tiles // X_CUTS) + j
+            span = slice(j * side_width, (j + 1) * side_width)
+            p_side(place).wait_recv()
+            for u in range(2):
+                cut_u = slice(u * own_rows + k * x_rows, u * own_rows + (k + 1) * x_rows)
+                res_v[cut_u, span] = (
+                    res_v[cut_u, span].astype(jnp.float32)
+                    + (proj_f[cut_u, span]
+                       + part_in[place, u * x_rows:(u + 1) * x_rows, :].astype(jnp.float32))
+                ).astype(jnp.bfloat16)
+        hid_sib(k).start()
+        at_k = slice(k * x_rows, (k + 1) * x_rows)
+        hid[s, at_k] = res_v[my_cut(s, k), :]
+        hid_sib(k).wait_recv()
+        h0 = hid[0, at_k].astype(jnp.float32)
+        h1 = hid[1, at_k].astype(jnp.float32)
+        square = jnp.sum(h0 * h0, axis=1, keepdims=True) + jnp.sum(h1 * h1, axis=1, keepdims=True)
+        inverse = lax.rsqrt(square / features + EPSILON)
+        rows[e, at_k, 0:half] = (h0 * inverse * g[0:1, 0:half]).astype(jnp.bfloat16)
+        rows[e, at_k, half:features] = (h1 * inverse * g[0:1, half:features]).astype(jnp.bfloat16)
+
+        @pl.when(has_up)
+        def _():
+            x_up(e, k).start()
+
+        @pl.when(has_down)
+        def _():
+            x_down(e, k).start()
+
+    w_from_part(4)
     units = 2 * wgu.shape[3]
     dims = (((1,), (1,)), ((), ()))
-    down_width = features // 4
-
-    def arrive(step):
-        n = slot_of(step, e, total)
-        below = n < e
-        x_up(n).wait_recv()
-
-        @pl.when(jnp.logical_and(below, has_up))
-        def _():
-            x_up(n).start()
-
-        @pl.when(jnp.logical_and(jnp.logical_not(below), has_down))
-        def _():
-            x_down(n).start()
-
-    middle = jnp.logical_and(has_up, has_down)
+    down_width = features // Z_CUTS
+
+    def turn(k):
+        return Z_CUTS // 2 * jnp.where(k < Z_CUTS // 2, 1 - s, s) + k % (Z_CUTS // 2)
+
+    def arrive_near(k):
+        @pl.when(middle)
+        def _():
+            x_up(e - 1, k).wait_recv()
+            x_up(e - 1, k).start()
+            x_down(e + 1, k).wait_recv()
+            x_down(e + 1, k).start()
+
+    def arrive(t):
+        @pl.when(jnp.logical_and(jnp.logical_not(middle), t > 0))
+        def _():
+            for k in range(X_CUTS):
+                x_up(slot_of(t, e, total), k).wait_recv()
+
+        @pl.when(t == 1)
+        def _():
+            for k in range(X_CUTS):
+                arrive_near(k)
+
+    def arrive_far(t):
+        for k in range(X_CUTS):
+            @pl.when(jnp.logical_and(middle, t == 1 + k))
+            def _():
+                @pl.when(low_side)
+                def _():
+                    x_down(last, k).wait_recv()
+                    x_down(last, k).start()
+
+                @pl.when(jnp.logical_not(low_side))
+                def _():
+                    x_up(0, k).wait_recv()
+                    x_up(0, k).start()
 
     def expert_step(t, carry):
         i = slot_of(t, e, total)
+
+        @pl.when(t == 0)
+        def _():
+            for piece in range(4):
+                for which in range(2):
+                    w_near(piece, which).wait_recv()
+
+        arrive(t)
         x = rows[i]
         activations = []
         for which in range(2):
@@ -652,22 +761,26 @@
             jnp.sum(jnp.where(gate_lane == 2 * e + which, gates_all, 0.0), axis=1, keepdims=True)
             for which in range(2)
         ]
+
+        arrive_far(t)
+
         @pl.when(t == 0)
         def _():
-            w_from_part(2)
+            w_from_part(5)
+            for piece in range(4, 6):
+                for which in range(2):
+                    w_near(piece, which).wait_recv()
+
+        for k in range(Z_CUTS):
+            c = turn(k)
+            mixed = None
             for which in range(2):
-                w_near(2, which).wait_recv()
-
-        for c in range(2):
-            for j in range(2):
-                span = slice((2 * c + j) * down_width, (2 * c + j + 1) * down_width)
-                mixed = None
-                for which in range(2):
-                    piece = weight[which] * jnp.dot(
-                        activations[which], wgu[which, 2, :, :, span].reshape(units, down_width),
-                        preferred_element_type=jnp.float32)
-                    mixed = piece if mixed is None else mixed + piece
-                results[i, c, :, j * down_width:(j + 1) * down_width] = mixed.astype(jnp.bfloat16)
+                piece = weight[which] * jnp.dot(
+                    activations[which],
+                    wgu[which, 2, :, :, col(c, down_width)].reshape(units, down_width),
+                    preferred_element_type=jnp.float32)
+                mixed = piece if mixed is None else mixed + piece
+            results[i, c] = mixed.astype(jnp.bfloat16)
 
             @pl.when(jnp.logical_and(i > e, jnp.logical_not(has_down)))
             def _():
@@ -676,14 +789,6 @@
             @pl.when(jnp.logical_and(i < e, jnp.logical_not(has_up)))
             def _():
                 z_down(i, c).start()
-
-        @pl.when(t < jnp.where(middle, 1, last))
-        def _():
-            arrive(t + 1)
-
-        @pl.when(jnp.logical_and(middle, t < last - 1))
-        def _():
-            arrive(t + 2)
         return carry
 
     lax.fori_loop(0, total, expert_step, 0)
@@ -694,37 +799,46 @@
             results[i, c].astype(jnp.float32) + chain_in[i, c].astype(jnp.float32)
         ).astype(jnp.bfloat16)
 
-    def pass_up(i):
-        @pl.when(jnp.logical_and(i <= last, has_down))
-        def _():
-            for c in range(2):
-                add_chain(i, c)
-                z_up(i, c).start()
-
-    def pass_down(i):
-        @pl.when(jnp.logical_and(i >= 0, has_up))
-        def _():
-            for c in range(2):
-                add_chain(i, c)
-                z_down(i, c).start()
-
-    low_side = e < total // 2
-    for phase in range(2):
-        def chain_step(j, carry):
-            up_now = low_side if phase == 0 else jnp.logical_not(low_side)
-
-            @pl.when(up_now)
-            def _():
-                pass_up(e + j)
-
-            @pl.when(jnp.logical_not(up_now))
-            def _():
-                pass_down(e - j)
-            return carry
-
-        lax.fori_loop(1, total, chain_step, 0)
-
-    for c in range(2):
+    def relay_up(i, k):
+        c = turn(k)
+        add_chain(i, c)
+        z_up(i, c).start()
+
+    def relay_down(i, k):
+        c = turn(k)
+        add_chain(i, c)
+        z_down(i, c).start()
+
+    @pl.when(jnp.logical_and(middle, low_side))
+    def _():
+        for k in range(Z_CUTS):
+            relay_up(e + 1, k)
+        for k in range(Z_CUTS + 2):
+            if k < Z_CUTS:
+                relay_up(last, k)
+            if k >= 2:
+                relay_down(0, k - 2)
+
+    @pl.when(jnp.logical_and(middle, jnp.logical_not(low_side)))
+    def _():
+        for k in range(Z_CUTS):
+            relay_down(e - 1, k)
+        for k in range(Z_CUTS + 2):
+            if k < Z_CUTS:
+                relay_down(0, k)
+            if k >= 2:
+                relay_up(last, k - 2)
+
+    def out_sib(q):
+        return sibling(23 + q, out_buf.at[0, q], out.at[s, :, pl.ds(q * down_width, down_width)])
+
+    def out_local(q):
+        return local(7 + q, out_buf.at[1, q], out.at[s, :, pl.ds(q * down_width, down_width)])
+
+    for k in range(Z_CUTS):
+        c = turn(k)
+        q = k % 2
+
         @pl.when(has_down)
         def _():
             z_up(e, c).wait_recv()
@@ -732,31 +846,28 @@
         @pl.when(has_up)
         def _():
             place = total + c * (total + 1)
-            remote(Z_UP, place, Z_IN, place, chain_in.at[total, c], chain_in.at[total, c],
-                   {"ep": e + 1}).wait_recv()
-
-    def side_sum(c):
+            block_ref = chain_in.at[total, c]
+            remote(Z_UP, 0, Z_IN, place, block_ref, block_ref, {"ep": e + 1}).wait_recv()
+        side = jnp.where(k < Z_CUTS // 2, 1 - s, s)
         value = results[e, c].astype(jnp.float32)
-        up_value = chain_in[e, c].astype(jnp.float32)
-        down_value = chain_in[total, c].astype(jnp.float32)
-        value = value + jnp.where(has_down, up_value, 0.0)
-        return value + jnp.where(has_up, down_value, 0.0)
-
-    first_half = (hid[0].astype(jnp.float32) + side_sum(0)).astype(jnp.bfloat16)
-    second_half = (hid[1].astype(jnp.float32) + side_sum(1)).astype(jnp.bfloat16)
-    is_first = s == 0
-    out[s] = jnp.where(is_first, first_half, second_half)
-    hid_out[...] = jnp.where(is_first, second_half, first_half)
-    out_sib = sibling(16, hid_out, out.at[s])
-    out_sib.start()
-    out_sib.wait_recv()
-
-    for piece in range(3):
+        value = value + jnp.where(has_down, chain_in[e, c].astype(jnp.float32), 0.0)
+        value = value + jnp.where(has_up, chain_in[total, c].astype(jnp.float32), 0.0)
+        value = hid[side, :, q * down_width:(q + 1) * down_width].astype(jnp.float32) + value
+        out_buf[k // 2, q] = value.astype(jnp.bfloat16)
+        if k < Z_CUTS // 2:
+            out_sib(q).start()
+        else:
+            out_local(q).start()
+    for q in range(2):
+        out_sib(q).wait_recv()
+        out_local(q).wait()
+
+    for piece in range(W_PIECES):
         w_side(piece).wait_send()
         w_part(piece).wait_send()
         w_near(piece, 0).wait_send()
         w_near(piece, 1).wait_send()
-    for copy in kv_sib + w_sib + [att_sib, att_own, hid_sib, out_sib]:
+    for copy in kv_sib + w_sib + [att_sib, att_own, hid_sib(0), hid_sib(1), out_sib(0), out_sib(1)]:
         copy.wait_send()
 
     def drain_tile(j, carry):
@@ -770,22 +881,24 @@
         def _():
             n_up(i).wait_send()
             c_up(i).wait_send()
-            x_up(i).wait_send()
+            for k in range(X_CUTS):
+                x_up(i, k).wait_send()
 
         @pl.when(jnp.logical_and(i >= e, has_down))
         def _():
             c_down(i).wait_send()
-            x_down(i).wait_send()
+            for k in range(X_CUTS):
+                x_down(i, k).wait_send()
 
         @pl.when(i > e)
         def _():
-            z_up(i, 0).wait_send()
-            z_up(i, 1).wait_send()
+            for c in range(Z_CUTS):
+                z_up(i, c).wait_send()
 
         @pl.when(i < e)
         def _():
-            z_down(i, 0).wait_send()
-            z_down(i, 1).wait_send()
+            for c in range(Z_CUTS):
+                z_down(i, c).wait_send()
         return carry
 
     lax.fori_loop(0, total, drain, 0)
@@ -805,7 +918,7 @@
     page_c, page = cache_keys.shape[0], new_keys.shape[0]
     hidden = w_down.shape[1]
     tiles = 4
-    slots = max(2 * (total + 1), tiles)
+    sent, arrived = (places[-1] for places in semaphore_places(total, tiles))
     anywhere = pl.BlockSpec(memory_space=pl.ANY)
     vmem = pl.BlockSpec(memory_space=pltpu.VMEM)
     bf, f32 = jnp.bfloat16, jnp.float32
@@ -814,7 +927,7 @@
         out_shape=jax.ShapeDtypeStruct((2, own_rows, half), bf),
         in_specs=[pl.BlockSpec(memory_space=pltpu.SMEM)] + [anywhere] * 7 + [vmem] + [anywhere] * 2
         + [vmem] * 2,
-        out_specs=pl.BlockSpec(memory_space=pltpu.VMEM),
+        out_specs=anywhere,
         scratch_shapes=[
             pltpu.VMEM((heads, query_rows, HD), bf),
             pltpu.VMEM((total, 2, 2 * page_c + 16, HD), bf),
@@ -824,21 +937,21 @@
             pltpu.VMEM((heads, query_rows, HD), f32),
             pltpu.VMEM((2, query_rows, heads * HD), bf),
             pltpu.VMEM(out_proj.shape, bf),
-            pltpu.VMEM((tiles, block_rows, half // tiles), bf),
-            pltpu.VMEM((tiles, block_rows, half // tiles), bf),
+            pltpu.VMEM((tiles, own_rows, half // 2), bf),
+            pltpu.VMEM((tiles, own_rows, half // 2), bf),
             pltpu.VMEM((block_rows, half), bf),
             pltpu.VMEM((2, own_rows, half), bf),
             pltpu.VMEM((2, 3, 2, hidden, features), bf),
             pltpu.VMEM((total, own_rows, features), bf),
-            pltpu.VMEM((total, 2, own_rows, half), bf),
-            pltpu.VMEM((total + 1, 2, own_rows, half), bf),
-            pltpu.SemaphoreType.DMA((10, slots)),
-            pltpu.SemaphoreType.DMA((7, slots)),
+            pltpu.VMEM((total, Z_CUTS, own_rows, features // Z_CUTS), bf),
+            pltpu.VMEM((total + 1, Z_CUTS, own_rows, features // Z_CUTS), bf),
+            pltpu.SemaphoreType.DMA((sent,)),
+            pltpu.SemaphoreType.DMA((arrived,)),
             pltpu.SemaphoreType.DMA((16 + heads,)),
             pltpu.SemaphoreType.DMA((SIB_COUNT,)),
             pltpu.SemaphoreType.DMA((SIB_COUNT,)),
-            pltpu.VMEM((tiles, block_rows, half // tiles), f32),
-            pltpu.VMEM((own_rows, half), bf),
+            pltpu.VMEM((block_rows, half), f32),
+            pltpu.VMEM((2, 2, own_rows, features // Z_CUTS), bf),
             pltpu.VMEM((total, 2 * own_rows, 128), f32),
         ],
         compiler_params=pltpu.CompilerParams(

time: 91.7 us -> 79.2 us (0.86)
  Pallas kernels: 89.1 us -> 76.7 us
    pallas_call x1, Pallas kernels: 89.1 us -> 76.7 us  [fused_shards(): pl.pallas_call(functools.partial(layer_kernel, total, tiles), out_shape=j...]
where the time goes in v2:
time: 79.2 us; the launch traced here: 79 us
  Pallas kernels  76.7 us (97%)
  local copies, waits for them, and re-layouts  1.67 us (2%)
    pallas_call x1, Pallas kernels, fused_shards(): pl.pallas_call(functools.partial(layer_kernel, total, tiles), out_shape=j...  76.7 us
    unnamed x1, local copies, waits for them, and re-layouts  1.67 us

profile of v2, /device:TPU:0, one launch (start us, length us, event | category | flops | bytes accessed | tf_op | source)
XLA Modules:
  0.0 79.0 jit_solution(8232309653939884215)
XLA Ops:
  0.7 76.7 %shard_map.127 = bf16[2,64,1024]{2,1,0:T(8,128)(2,1)} custom-call(s32[1]{0:T(128)S(6)} %copy.15.page_len, bf16[256,2048]{1,0:T(8,128)(2,1)} %queries.1, bf16[128,512]{1,0:T(8,128)(2,1)} %cache_keys.1, bf16[128,512]{1,0:T(8,128)(2,1)} %cache_values.1, bf16[128,512]{1,0:T(8,128)(2,1)} %new_keys.1, bf16[128,512]{1,0:T(8,128)(2,1)} %new_values.1, ...), custom_call_target="tpu_custom_call" | custom-call | tf_op jit(solution)/shard_map/pallas_call | solution.py:925
  77.4 1.7 %copy.16 = bf16[128,1024]{1,0:T(8,128)(2,1)} copy(bf16[128,1024]{1,0:T(8,128)(2,1)} %bitcast.3) | data formatting | bytes 524288

commit v3 on v2

--- a/solution.py
+++ b/solution.py
@@ -260,12 +260,12 @@
 
 def layer_kernel(
     total, tiles,
-    page_len, queries, cache_keys, cache_values, new_keys, new_values, out_proj, residual, gain_v,
+    page_len, queries, cache_keys, cache_values, new_keys, new_values, out_proj, residual, gain,
     gate_up, w_down, ids_t, gates_t,
     out,
     q_v, cbuf, nbuf, m_v, l_v, acc_v, att, proj_w, part_out, part_in, res_v, hid, wgu,
     rows, results, chain_in,
-    send_sem, recv_sem, load_sem, sib_send, sib_recv, proj_f, out_buf, gate_cols,
+    send_sem, recv_sem, load_sem, sib_send, sib_recv, proj_f, out_buf, gate_cols, ids_v, gates_v, gain_v,
 ):
     e = lax.axis_index("ep")
     h = lax.axis_index("hd")
@@ -289,6 +289,19 @@
     def local(index, src, dst):
         return pltpu.make_async_copy(src, dst, load_sem.at[index])
 
+    barrier = pltpu.get_barrier_semaphore()
+    pl.semaphore_signal(barrier, inc=1, device_id={"sub": 1 - s}, device_id_type=MESH)
+    pl.semaphore_signal(barrier, inc=1, device_id={"hd": 1 - h}, device_id_type=MESH)
+    pl.semaphore_signal(barrier, inc=1, device_id={"grp": 1 - part}, device_id_type=MESH)
+
+    @pl.when(has_up)
+    def _():
+        pl.semaphore_signal(barrier, inc=1, device_id={"ep": e + 1}, device_id_type=MESH)
+
+    @pl.when(has_down)
+    def _():
+        pl.semaphore_signal(barrier, inc=1, device_id={"ep": e - 1}, device_id_type=MESH)
+
     mine = 2 * h + s
     loads = [
         local(0, cache_keys.at[:, col(mine, HD)], cbuf.at[e, s, pl.ds(0, page_c)]),
@@ -305,14 +318,17 @@
         local(9, gate_up.at[0], wgu.at[h, pl.ds(0, 2), s]),
         local(10, w_down.at[0], wgu.at[h, 2, s]),
     ]
-    for copy in loads + q_loads + w_loads:
+    small_loads = [local(2, ids_t, ids_v), local(11, gates_t, gates_v), local(12, gain, gain_v)]
+    for copy in small_loads + loads + q_loads + w_loads:
         copy.start()
 
     experts = 2 * total
     lane = lax.broadcasted_iota(jnp.int32, (8, HD), 1)
     seen = jnp.where(lane < page_len[0], 0.0, NEG_FILL)
-    ids = ids_t[...]
-    gate_values = gates_t[...].astype(jnp.float32)
+    for copy in small_loads:
+        copy.wait()
+    ids = ids_v[...]
+    gate_values = gates_v[...].astype(jnp.float32)
     place = lax.broadcasted_iota(jnp.int32, (8, HD), 0)
     by_expert = jnp.zeros((8, HD), jnp.float32)
     for x in range(experts):
@@ -320,19 +336,6 @@
         by_expert = jnp.where(place == x, one_row, by_expert)
     cbuf[e, s, 2 * page_c:2 * page_c + 16, :] = jnp.concatenate(
         [seen, by_expert], axis=0).astype(jnp.bfloat16)
-
-    barrier = pltpu.get_barrier_semaphore()
-    pl.semaphore_signal(barrier, inc=1, device_id={"sub": 1 - s}, device_id_type=MESH)
-    pl.semaphore_signal(barrier, inc=1, device_id={"hd": 1 - h}, device_id_type=MESH)
-    pl.semaphore_signal(barrier, inc=1, device_id={"grp": 1 - part}, device_id_type=MESH)
-
-    @pl.when(has_up)
-    def _():
-        pl.semaphore_signal(barrier, inc=1, device_id={"ep": e + 1}, device_id_type=MESH)
-
-    @pl.when(has_down)
-    def _():
-        pl.semaphore_signal(barrier, inc=1, device_id={"ep": e - 1}, device_id_type=MESH)
 
     pl.semaphore_wait(barrier, 3 + has_up.astype(jnp.int32) + has_down.astype(jnp.int32))
 
@@ -830,10 +833,7 @@
                 relay_up(last, k - 2)
 
     def out_sib(q):
-        return sibling(23 + q, out_buf.at[0, q], out.at[s, :, pl.ds(q * down_width, down_width)])
-
-    def out_local(q):
-        return local(7 + q, out_buf.at[1, q], out.at[s, :, pl.ds(q * down_width, down_width)])
+        return sibling(23 + q, out_buf.at[q], out.at[s, :, pl.ds(q * down_width, down_width)])
 
     for k in range(Z_CUTS):
         c = turn(k)
@@ -853,14 +853,13 @@
         value = value + jnp.where(has_down, chain_in[e, c].astype(jnp.float32), 0.0)
         value = value + jnp.where(has_up, chain_in[total, c].astype(jnp.float32), 0.0)
         value = hid[side, :, q * down_width:(q + 1) * down_width].astype(jnp.float32) + value
-        out_buf[k // 2, q] = value.astype(jnp.bfloat16)
         if k < Z_CUTS // 2:
+            out_buf[q] = value.astype(jnp.bfloat16)
             out_sib(q).start()
         else:
-            out_local(q).start()
+            out[s, :, q * down_width:(q + 1) * down_width] = value.astype(jnp.bfloat16)
     for q in range(2):
         out_sib(q).wait_recv()
-        out_local(q).wait()
 
     for piece in range(W_PIECES):
         w_side(piece).wait_send()
@@ -920,14 +919,13 @@
     tiles = 4
     sent, arrived = (places[-1] for places in semaphore_places(total, tiles))
     anywhere = pl.BlockSpec(memory_space=pl.ANY)
-    vmem = pl.BlockSpec(memory_space=pltpu.VMEM)
     bf, f32 = jnp.bfloat16, jnp.float32
+    ids_rows, gate_rows = expert_ids.T, gates.T
     out = pl.pallas_call(
         functools.partial(layer_kernel, total, tiles),
-        out_shape=jax.ShapeDtypeStruct((2, own_rows, half), bf),
-        in_specs=[pl.BlockSpec(memory_space=pltpu.SMEM)] + [anywhere] * 7 + [vmem] + [anywhere] * 2
-        + [vmem] * 2,
-        out_specs=anywhere,
+        out_shape=pltpu.VMEM((2, own_rows, half), bf),
+        in_specs=[pl.BlockSpec(memory_space=pltpu.SMEM)] + [anywhere] * 12,
+        out_specs=pl.BlockSpec(memory_space=pltpu.VMEM),
         scratch_shapes=[
             pltpu.VMEM((heads, query_rows, HD), bf),
             pltpu.VMEM((total, 2, 2 * page_c + 16, HD), bf),
@@ -951,14 +949,17 @@
             pltpu.SemaphoreType.DMA((SIB_COUNT,)),
             pltpu.SemaphoreType.DMA((SIB_COUNT,)),
             pltpu.VMEM((block_rows, half), f32),
-            pltpu.VMEM((2, 2, own_rows, features // Z_CUTS), bf),
+            pltpu.VMEM((2, own_rows, features // Z_CUTS), bf),
             pltpu.VMEM((total, 2 * own_rows, 128), f32),
+            pltpu.VMEM(ids_rows.shape, jnp.int32),
+            pltpu.VMEM(gate_rows.shape, bf),
+            pltpu.VMEM(norm_gain.shape, bf),
         ],
         compiler_params=pltpu.CompilerParams(
             collective_id=0, has_side_effects=True, vmem_limit_bytes=58 * 1024 * 1024
         ),
     )(page_len, queries, cache_keys, cache_values, new_keys, new_values, out_proj, residual,
-      norm_gain, gate_up, w_down, expert_ids.T, gates.T)
+      norm_gain, gate_up, w_down, ids_rows, gate_rows)
     return out.reshape(block_rows, half)
 
 

time: 79.2 us -> 76.8 us (0.970)
  Pallas kernels: 76.7 us -> 75.3 us
  local copies, waits for them, and re-layouts: 1.67 us -> 0.71 us
    pallas_call x1, Pallas kernels: 76.7 us -> 75.3 us  [fused_shards(): pl.pallas_call(functools.partial(layer_kernel, total, tiles), out_shape=p...]
    unnamed x1, local copies, waits for them, and re-layouts: 1.67 us -> 0.71 us
where the time goes in v3:
time: 76.8 us; the launch traced here: 76.7 us
  Pallas kernels  75.3 us (98%)
    pallas_call x1, Pallas kernels, fused_shards(): pl.pallas_call(functools.partial(layer_kernel, total, tiles), out_shape=p...  75.3 us

profile of v3, /device:TPU:0, one launch (start us, length us, event | category | flops | bytes accessed | tf_op | source)
XLA Modules:
  0.0 76.7 jit_solution(666511060638016621)
XLA Ops:
  0.7 75.3 %shard_map.127 = bf16[2,64,1024]{2,1,0:T(8,128)(2,1)S(1)} custom-call(s32[1]{0:T(128)S(6)} %copy.16.page_len, bf16[256,2048]{1,0:T(8,128)(2,1)} %queries.1, bf16[128,512]{1,0:T(8,128)(2,1)} %cache_keys.1, bf16[128,512]{1,0:T(8,128)(2,1)} %cache_values.1, bf16[128,512]{1,0:T(8,128)(2,1)} %new_keys.1, bf16[128,512]{1,0:T(8,128)(2,1)} %new_values.1, ...), custom_call_target="tpu_custom_call" | custom-call | tf_op jit(solution)/shard_map/pallas_call | solution.py:924
  75.9 0.7 copy.15

commit v4 on v3

--- a/solution.py
+++ b/solution.py
@@ -244,7 +244,7 @@
 
 (C_UP, C_DOWN, N_UP, X_UP, X_DOWN, W_SIDE, W_PART, Z_UP, Z_DOWN, P_SIDE) = range(10)
 (C_IN, N_IN, X_IN, W_SIDE_IN, W_PART_IN, Z_IN, P_IN) = range(7)
-SIB_COUNT = 25
+SIB_COUNT = 15
 W_PIECES = 6
 X_CUTS = 2
 Z_CUTS = 4
@@ -252,10 +252,8 @@
 
 
 def semaphore_places(total, tiles):
-    sent = (total, total, total, X_CUTS * total, X_CUTS * total, W_PIECES, W_PIECES,
-            Z_CUTS * total, Z_CUTS * total, tiles)
     arrived = (total, total, X_CUTS * total, W_PIECES, W_PIECES, Z_CUTS * (total + 1), tiles)
-    return [[sum(sizes[:i]) for i in range(len(sizes) + 1)] for sizes in (sent, arrived)]
+    return [sum(arrived[:i]) for i in range(len(arrived) + 1)]
 
 
 def layer_kernel(
@@ -280,7 +278,7 @@
     features = 2 * half
     scale = LOG2_E / math.sqrt(HD)
     has_up = e < last
-    sent_at, arrived_at = semaphore_places(total, tiles)
+    arrived_at = semaphore_places(total, tiles)
     has_down = e > 0
 
     def col(index, width):
@@ -301,6 +299,9 @@
     @pl.when(has_down)
     def _():
         pl.semaphore_signal(barrier, inc=1, device_id={"ep": e - 1}, device_id_type=MESH)
+
+    def whole(ref, semaphore):
+        pltpu.make_async_copy(ref, ref, semaphore).wait()
 
     mine = 2 * h + s
     loads = [
@@ -310,7 +311,7 @@
         local(4, new_values.at[:, col(mine, HD)], nbuf.at[e, s, pl.ds(page, page)]),
     ]
     q_loads = [
-        local(16 + i, queries.at[:, col(s * heads + i, HD)], q_v.at[i]) for i in range(heads)
+        local(13, queries.at[:, col(s * heads + i, HD)], q_v.at[i]) for i in range(heads)
     ]
     w_loads = [
         local(5, out_proj, proj_w),
@@ -339,14 +340,15 @@
 
     pl.semaphore_wait(barrier, 3 + has_up.astype(jnp.int32) + has_down.astype(jnp.int32))
 
-    def sibling(index, src, dst):
+    def sibling(index, src, dst, arrival=None):
         return pltpu.make_async_remote_copy(
-            src_ref=src, dst_ref=dst, send_sem=sib_send.at[index], recv_sem=sib_recv.at[index],
+            src_ref=src, dst_ref=dst, send_sem=sib_send.at[index],
+            recv_sem=sib_recv.at[index if arrival is None else arrival],
             device_id={"sub": 1 - s}, device_id_type=MESH)
 
     def remote(kind, index, arrival, slot, src, dst, where):
         return pltpu.make_async_remote_copy(
-            src_ref=src, dst_ref=dst, send_sem=send_sem.at[sent_at[kind] + index],
+            src_ref=src, dst_ref=dst, send_sem=send_sem.at[kind],
             recv_sem=recv_sem.at[arrived_at[arrival] + slot], device_id=where, device_id_type=MESH)
 
     theirs = 2 * h + 1 - s
@@ -386,7 +388,7 @@
 
     def w_near(piece, which):
         block_ref = w_block(piece, jnp.where(which == 0, part, 1 - part))
-        return sibling(11 + 2 * piece + which, block_ref, block_ref)
+        return sibling(11, block_ref, block_ref, 11 + piece // 4)
 
     def w_from_side(piece):
         block_ref = w_block(piece, part)
@@ -426,8 +428,7 @@
 
     for copy in w_sib:
         copy.start()
-    for copy in q_loads:
-        copy.wait()
+    whole(q_v, load_sem.at[13])
 
     def parts_of(buf, index, size):
         return (buf[index, :, 0:size, :].reshape(2 * size, HD),
@@ -572,19 +573,24 @@
             [flat, jnp.zeros((HD - 8, HD), jnp.float32)], axis=0).T
         return carry
 
-    def finish_head(i, carry):
-        att[s, :, col(i, HD)] = (
-            acc_v[i] / jnp.sum(l_v[i], axis=1, keepdims=True)).astype(jnp.bfloat16)
-        return carry
-
-    lax.fori_loop(0, heads, finish_head, 0)
     block = 2 * own_rows
 
+    def block_at(which):
+        return pl.ds(pl.multiple_of(which * block, block), block)
+
     def att_rows(which):
-        return att.at[s, pl.ds(pl.multiple_of(which * block, block), block)]
-
+        return att.at[s, block_at(which)]
+
+    def finish(which):
+        for i in range(heads):
+            att[s, block_at(which), i * HD:(i + 1) * HD] = (
+                acc_v[i, block_at(which), :]
+                / jnp.sum(l_v[i, block_at(which), :], axis=1, keepdims=True)).astype(jnp.bfloat16)
+
+    finish(1 - h)
     att_sib = sibling(7, att_rows(1 - h), att_rows(1 - h))
     att_sib.start()
+    finish(h)
     att_own = sibling(9, att_rows(h), att_rows(h))
     att_own.start()
     for copy in w_loads[:2]:
@@ -744,9 +750,7 @@
 
         @pl.when(t == 0)
         def _():
-            for piece in range(4):
-                for which in range(2):
-                    w_near(piece, which).wait_recv()
+            whole(wgu.at[1 - h, pl.ds(0, 2), s], sib_recv.at[11])
 
         arrive(t)
         x = rows[i]
@@ -770,9 +774,7 @@
         @pl.when(t == 0)
         def _():
             w_from_part(5)
-            for piece in range(4, 6):
-                for which in range(2):
-                    w_near(piece, which).wait_recv()
+            whole(wgu.at[1 - h, 2, s], sib_recv.at[12])
 
         for k in range(Z_CUTS):
             c = turn(k)
@@ -833,7 +835,7 @@
                 relay_up(last, k - 2)
 
     def out_sib(q):
-        return sibling(23 + q, out_buf.at[q], out.at[s, :, pl.ds(q * down_width, down_width)])
+        return sibling(13 + q, out_buf.at[q], out.at[s, :, pl.ds(q * down_width, down_width)])
 
     for k in range(Z_CUTS):
         c = turn(k)
@@ -861,46 +863,23 @@
     for q in range(2):
         out_sib(q).wait_recv()
 
-    for piece in range(W_PIECES):
-        w_side(piece).wait_send()
-        w_part(piece).wait_send()
-        w_near(piece, 0).wait_send()
-        w_near(piece, 1).wait_send()
+    whole(wgu.at[h, :, s, pl.ds(0, cut)], send_sem.at[W_SIDE])
+    whole(wgu.at[h, :, s, pl.ds(0, cut)], send_sem.at[W_PART])
+    whole(wgu.at[1 - h, :, s], sib_send.at[11])
+    whole(part_out, send_sem.at[P_SIDE])
     for copy in kv_sib + w_sib + [att_sib, att_own, hid_sib(0), hid_sib(1), out_sib(0), out_sib(1)]:
         copy.wait_send()
 
-    def drain_tile(j, carry):
-        p_side(j).wait_send()
-        return carry
-
-    lax.fori_loop(0, tiles, drain_tile, 0)
-
-    def drain(i, carry):
-        @pl.when(jnp.logical_and(i <= e, has_up))
-        def _():
-            n_up(i).wait_send()
-            c_up(i).wait_send()
-            for k in range(X_CUTS):
-                x_up(i, k).wait_send()
-
-        @pl.when(jnp.logical_and(i >= e, has_down))
-        def _():
-            c_down(i).wait_send()
-            for k in range(X_CUTS):
-                x_down(i, k).wait_send()
-
-        @pl.when(i > e)
-        def _():
-            for c in range(Z_CUTS):
-                z_up(i, c).wait_send()
-
-        @pl.when(i < e)
-        def _():
-            for c in range(Z_CUTS):
-                z_down(i, c).wait_send()
-        return carry
-
-    lax.fori_loop(0, total, drain, 0)
+    for i in range(total):
+        sends_up = [(N_UP, nbuf, i + 1), (C_UP, cbuf, i + 1), (X_UP, rows, i + 1),
+                    (Z_UP, results, last - i)]
+        sends_down = [(C_DOWN, cbuf, total - i), (X_DOWN, rows, total - i), (Z_DOWN, results, i)]
+        sends = (sends_up if i < last else []) + (sends_down if i > 0 else [])
+
+        @pl.when(e == i)
+        def _():
+            for kind, ref, count in sends:
+                whole(ref.at[pl.ds(0, count)], send_sem.at[kind])
 
 
 def fused_shards(
@@ -917,7 +896,7 @@
     page_c, page = cache_keys.shape[0], new_keys.shape[0]
     hidden = w_down.shape[1]
     tiles = 4
-    sent, arrived = (places[-1] for places in semaphore_places(total, tiles))
+    arrived = semaphore_places(total, tiles)[-1]
     anywhere = pl.BlockSpec(memory_space=pl.ANY)
     bf, f32 = jnp.bfloat16, jnp.float32
     ids_rows, gate_rows = expert_ids.T, gates.T
@@ -943,9 +922,9 @@
             pltpu.VMEM((total, own_rows, features), bf),
             pltpu.VMEM((total, Z_CUTS, own_rows, features // Z_CUTS), bf),
             pltpu.VMEM((total + 1, Z_CUTS, own_rows, features // Z_CUTS), bf),
-            pltpu.SemaphoreType.DMA((sent,)),
+            pltpu.SemaphoreType.DMA((10,)),
             pltpu.SemaphoreType.DMA((arrived,)),
-            pltpu.SemaphoreType.DMA((16 + heads,)),
+            pltpu.SemaphoreType.DMA((14,)),
             pltpu.SemaphoreType.DMA((SIB_COUNT,)),
             pltpu.SemaphoreType.DMA((SIB_COUNT,)),
             pltpu.VMEM((block_rows, half), f32),

time: 76.8 us -> 75.8 us (0.987)
  Pallas kernels: 75.3 us -> 74.2 us
    pallas_call x1, Pallas kernels: 75.3 us -> 74.2 us  [fused_shards(): pl.pallas_call(functools.partial(layer_kernel, total, tiles), out_shape=p...]
where the time goes in v4:
time: 75.8 us; the launch traced here: 75.6 us
  Pallas kernels  74.2 us (98%)
    pallas_call x1, Pallas kernels, fused_shards(): pl.pallas_call(functools.partial(layer_kernel, total, tiles), out_shape=p...  74.2 us

profile of v4, /device:TPU:0, one launch (start us, length us, event | category | flops | bytes accessed | tf_op | source)
XLA Modules:
  0.0 75.6 jit_solution(7094468715961901502)
XLA Ops:
  0.7 74.2 %shard_map.127 = bf16[2,64,1024]{2,1,0:T(8,128)(2,1)S(1)} custom-call(s32[1]{0:T(128)S(6)} %copy.16.page_len, bf16[256,2048]{1,0:T(8,128)(2,1)} %queries.1, bf16[128,512]{1,0:T(8,128)(2,1)} %cache_keys.1, bf16[128,512]{1,0:T(8,128)(2,1)} %cache_values.1, bf16[128,512]{1,0:T(8,128)(2,1)} %new_keys.1, bf16[128,512]{1,0:T(8,128)(2,1)} %new_values.1, ...), custom_call_target="tpu_custom_call" | custom-call | tf_op jit(solution)/shard_map/pallas_call | solution.py:903
  74.9 0.7 copy.15

commit v5 on v4

--- a/solution.py
+++ b/solution.py
@@ -757,11 +757,11 @@
         activations = []
         for which in range(2):
             gate_part = lax.dot_general(
-                x, wgu[which, 0].reshape(units, features), dims, preferred_element_type=jnp.float32)
+                wgu[which, 0].reshape(units, features), x, dims, preferred_element_type=jnp.float32)
             up_part = lax.dot_general(
-                x, wgu[which, 1].reshape(units, features), dims, preferred_element_type=jnp.float32)
+                wgu[which, 1].reshape(units, features), x, dims, preferred_element_type=jnp.float32)
             activations.append(
-                (gate_part / (1.0 + jnp.exp(-gate_part)) * up_part).astype(jnp.bfloat16))
+                (gate_part / (1.0 + jnp.exp(-gate_part)) * up_part).T.astype(jnp.bfloat16))
         gates_all = gate_cols[i, my_rows(s), :]
         gate_lane = lax.broadcasted_iota(jnp.int32, gates_all.shape, 1)
         weight = [

time: 75.8 us -> 75.7 us (level)
  no operation moved by 1% of the time
where the time goes in v5:
time: 75.7 us; the launch traced here: 75.5 us
  Pallas kernels  74.1 us (98%)
    pallas_call x1, Pallas kernels, fused_shards(): pl.pallas_call(functools.partial(layer_kernel, total, tiles), out_shape=p...  74.1 us

profile of v5, /device:TPU:0, one launch (start us, length us, event | category | flops | bytes accessed | tf_op | source)
XLA Modules:
  0.0 75.5 jit_solution(5138528436337611241)
XLA Ops:
  0.7 74.1 %shard_map.127 = bf16[2,64,1024]{2,1,0:T(8,128)(2,1)S(1)} custom-call(s32[1]{0:T(128)S(6)} %copy.16.page_len, bf16[256,2048]{1,0:T(8,128)(2,1)} %queries.1, bf16[128,512]{1,0:T(8,128)(2,1)} %cache_keys.1, bf16[128,512]{1,0:T(8,128)(2,1)} %cache_values.1, bf16[128,512]{1,0:T(8,128)(2,1)} %new_keys.1, bf16[128,512]{1,0:T(8,128)(2,1)} %new_values.1, ...), custom_call_target="tpu_custom_call" | custom-call | tf_op jit(solution)/shard_map/pallas_call | solution.py:903
  74.8 0.7 copy.15

commit v6 on v5

--- a/solution.py
+++ b/solution.py
@@ -537,7 +537,7 @@
         def _():
             w_from_side(0)
 
-        @pl.when(jnp.logical_and(t == 3, jnp.logical_not(middle)))
+        @pl.when(jnp.logical_and(t == 3, jnp.logical_not(has_up)))
         def _():
             w_from_side(3)
 
@@ -559,7 +559,7 @@
 
         @pl.when(t == 3)
         def _():
-            @pl.when(middle)
+            @pl.when(has_up)
             def _():
                 w_from_side(3)
             w_from_part(0)

time: 75.7 us -> 75.7 us (level)
  no operation moved by 1% of the time
where the time goes in v6:
time: 75.7 us; the launch traced here: 75.5 us
  Pallas kernels  74.1 us (98%)
    pallas_call x1, Pallas kernels, fused_shards(): pl.pallas_call(functools.partial(layer_kernel, total, tiles), out_shape=p...  74.1 us

profile of v6, /device:TPU:0, one launch (start us, length us, event | category | flops | bytes accessed | tf_op | source)
XLA Modules:
  0.0 75.5 jit_solution(6216500103112677087)
XLA Ops:
  0.7 74.1 %shard_map.127 = bf16[2,64,1024]{2,1,0:T(8,128)(2,1)S(1)} custom-call(s32[1]{0:T(128)S(6)} %copy.16.page_len, bf16[256,2048]{1,0:T(8,128)(2,1)} %queries.1, bf16[128,512]{1,0:T(8,128)(2,1)} %cache_keys.1, bf16[128,512]{1,0:T(8,128)(2,1)} %cache_values.1, bf16[128,512]{1,0:T(8,128)(2,1)} %new_keys.1, bf16[128,512]{1,0:T(8,128)(2,1)} %new_values.1, ...), custom_call_target="tpu_custom_call" | custom-call | tf_op jit(solution)/shard_map/pallas_call | solution.py:903
  74.8 0.7 copy.15
